TPU v7x, 512 devices: a whole 4x4x16 slice. The times are simulated.
512 devices in a mesh: sensor: 128 (over y, z, core), step: 4 (over x).
Axes of the slice: x: 4, y: 4, z: 16, core: 2. Of those that a mesh axis runs over, the one named last changes fastest.
Arguments:
- inputs: bfloat16 [12, 8192, 512], P('step', 'sensor'), may hold values from -6 to 6
- cotangent: bfloat16 [12, 8192, 512], P('step', 'sensor'), may hold values from -6 to 6
- w_query: bfloat16 [512, 512], replicated, may hold values from -0.25 to 0.25
- w_key: bfloat16 [512, 512], replicated, may hold values from -0.25 to 0.25
- w_value: bfloat16 [512, 512], replicated, may hold values from -0.25 to 0.25
- w_up: bfloat16 [512, 256], replicated, may hold values from -0.25 to 0.25
- w_down: bfloat16 [256, 512], replicated, may hold values from -0.375 to 0.375
- feature_proj: float32 [8, 64, 64], replicated, may hold values from -5 to 5
- live_count: int32 [128], P('sensor'), may hold values from 32 to 64, as said below
Outputs:
- grad_inputs: bfloat16 [12, 8192, 512], P('step', 'sensor')
- grad_query: float32 [512, 512], P('sensor', 'step')
- grad_key: float32 [512, 512], P('sensor', 'step')
- grad_value: float32 [512, 512], P('sensor', 'step')
Inputs may be any that keep to these rules, and one draw needn't show every extreme that they name: `live_count`: some group has all 64 sensors live; every group has at least half of them live.
All inputs are finite; a program needn't handle non-finite values.
Results may differ from a plain program's by a relative error of at most 0.012.
Values sent between devices are 32-bit elements; how exact they have to be, the bound alone decides.
A program may use at most 64 MiB of HBM per device.

v0:
```python
import math

import jax
import jax.numpy as jnp
from jax import lax
from jax.sharding import PartitionSpec as P

HIGH = lax.Precision.HIGHEST


def feature_map(scaled, feature_proj):
    projected = jnp.einsum("...he,her->...hr", scaled, feature_proj, precision=HIGH)
    return jnp.exp(
        projected - 0.5 * jnp.sum(scaled * scaled, -1, keepdims=True)
    ) * feature_proj.shape[2] ** (-0.5)


def feature_back(incoming, feat, scaled, feature_proj):
    weighted = incoming * feat
    return jnp.einsum(
        "...hr,her->...he", weighted, feature_proj, precision=HIGH
    ) - scaled * jnp.sum(weighted, -1, keepdims=True)


def shards(inputs, cotangent, w_query, w_key, w_value, w_up, w_down, feature_proj, live_count):
    steps_here, sensors_here, width = inputs.shape
    heads, head_dim, feats = feature_proj.shape
    factor = head_dim ** (-0.25)
    valid = (jnp.arange(sensors_here, dtype=jnp.int32) < live_count[0]).astype(jnp.float32)
    flat_in = inputs.reshape(steps_here * sensors_here, width)

    def project(weight):
        return jnp.dot(flat_in, weight, preferred_element_type=jnp.float32).reshape(
            steps_here, sensors_here, heads, head_dim
        )

    scaled_query = project(w_query) * factor
    scaled_key = project(w_key) * factor
    values = project(w_value)
    feat_query = feature_map(scaled_query, feature_proj)
    feat_key = feature_map(scaled_key, feature_proj)
    masked_key = feat_key * valid[None, :, None, None]
    local_summary = jnp.einsum("tnhr,tnhe->thre", masked_key, values, precision=HIGH)
    local_normal = jnp.sum(masked_key, 1)
    summed = [
        lax.psum((local_summary[moment], local_normal[moment]), "sensor")
        for moment in range(steps_here)
    ]
    summary = jnp.stack([entry[0] for entry in summed])
    normal_sum = jnp.stack([entry[1] for entry in summed])
    numer = jnp.einsum("tnhr,thre->tnhe", feat_query, summary, precision=HIGH)
    denom = jnp.einsum("tnhr,thr->tnh", feat_query, normal_sum, precision=HIGH)
    attended = numer / denom[..., None]
    flat_att = attended.reshape(steps_here * sensors_here, width)
    rms_val = jnp.sqrt(jnp.mean(flat_att * flat_att, -1, keepdims=True) + 1e-06)
    normed = flat_att / rms_val
    pre_act = jnp.dot(normed.astype(jnp.bfloat16), w_up, preferred_element_type=jnp.float32)
    masked_cot = (cotangent * valid.astype(jnp.bfloat16)[None, :, None]).reshape(
        steps_here * sensors_here, width
    )
    grad_hidden = jnp.dot(masked_cot, w_down.T, preferred_element_type=jnp.float32)
    _, gelu_back = jax.vjp(jax.nn.gelu, pre_act)
    grad_pre = gelu_back(grad_hidden)[0].astype(jnp.bfloat16)
    grad_normed = jnp.dot(grad_pre, w_up.T, preferred_element_type=jnp.float32)
    grad_att = (grad_normed - normed * jnp.mean(grad_normed * normed, -1, keepdims=True)) / rms_val
    grad_att = grad_att.reshape(steps_here, sensors_here, heads, head_dim)
    grad_num = grad_att / denom[..., None]
    grad_den = -jnp.sum(grad_att * attended, -1) / denom
    grad_fq = (
        jnp.einsum("tnhe,thre->tnhr", grad_num, summary, precision=HIGH)
        + grad_den[..., None] * normal_sum[:, None]
    )
    local_gsum = jnp.einsum("tnhr,tnhe->thre", feat_query, grad_num, precision=HIGH)
    local_gnorm = jnp.einsum("tnhr,tnh->thr", feat_query, grad_den, precision=HIGH)
    gathered = [
        lax.psum((local_gsum[moment], local_gnorm[moment]), "sensor")
        for moment in range(steps_here)
    ]
    grad_summary = jnp.stack([entry[0] for entry in gathered])
    grad_normal = jnp.stack([entry[1] for entry in gathered])
    grad_fk = (
        jnp.einsum("tnhe,thre->tnhr", values, grad_summary, precision=HIGH) + grad_normal[:, None]
    ) * valid[None, :, None, None]
    grad_val = jnp.einsum("tnhr,thre->tnhe", masked_key, grad_summary, precision=HIGH)
    grad_q = feature_back(grad_fq, feat_query, scaled_query, feature_proj) * factor
    grad_k = feature_back(grad_fk, feat_key, scaled_key, feature_proj) * factor
    flat_rows = steps_here * sensors_here
    grad_q = grad_q.reshape(flat_rows, width).astype(jnp.bfloat16)
    grad_k = grad_k.reshape(flat_rows, width).astype(jnp.bfloat16)
    grad_val = grad_val.reshape(flat_rows, width).astype(jnp.bfloat16)
    grad_in = jnp.dot(grad_q, w_query.T, preferred_element_type=jnp.float32)
    grad_in = grad_in + jnp.dot(grad_k, w_key.T, preferred_element_type=jnp.float32)
    grad_in = grad_in + jnp.dot(grad_val, w_value.T, preferred_element_type=jnp.float32)
    grad_inputs = grad_in.astype(jnp.bfloat16).reshape(steps_here, sensors_here, width)
    weight_q = jnp.einsum("nd,nk->dk", flat_in, grad_q, preferred_element_type=jnp.float32)
    weight_k = jnp.einsum("nd,nk->dk", flat_in, grad_k, preferred_element_type=jnp.float32)
    weight_v = jnp.einsum("nd,nk->dk", flat_in, grad_val, preferred_element_type=jnp.float32)
    partial_sums = (
        lax.psum_scatter(weight_q, "sensor", scatter_dimension=0, tiled=True),
        lax.psum_scatter(weight_k, "sensor", scatter_dimension=0, tiled=True),
        lax.psum_scatter(weight_v, "sensor", scatter_dimension=0, tiled=True),
    )
    reduced = (
        lax.psum_scatter(partial_sums[0], "step", scatter_dimension=1, tiled=True),
        lax.psum_scatter(partial_sums[1], "step", scatter_dimension=1, tiled=True),
        lax.psum_scatter(partial_sums[2], "step", scatter_dimension=1, tiled=True),
    )
    total_rows = steps_here * lax.axis_size("step") * sensors_here * lax.axis_size("sensor")
    norm_scale = 1.0 / math.sqrt(total_rows)
    return (grad_inputs, reduced[0] * norm_scale, reduced[1] * norm_scale, reduced[2] * norm_scale)


def solution(mesh):
    placed = (
        P("step", "sensor", None),
        P("step", "sensor", None),
        P(),
        P(),
        P(),
        P(),
        P(),
        P(),
        P("sensor"),
    )
    return jax.shard_map(
        shards,
        mesh=mesh,
        in_specs=placed,
        out_specs=(
            P("step", "sensor", None),
            P("sensor", "step"),
            P("sensor", "step"),
            P("sensor", "step"),
        ),
        check_vma=False,
    )
```

profile of v0, /device:TPU:1, one launch (start us, length us, event | category | flops | bytes accessed | tf_op | source)
XLA Modules:
  0.0 1836.7 jit_solution(7626119864495124571)
XLA Ops:
  9.2 1.4 multiply_reduce_fusion.3
  11.3 2.5 fusion.76
  13.7 1.4 fusion.28
  17.3 1.4 multiply_reduce_fusion.2
  19.2 1.5 fusion.4
  20.7 498.4 %all-reduce.4 = (f32[1,8,64]{2,0,1:T(1,128)S(1)}, f32[1,8,64]{2,0,1:T(1,128)S(1)}, f32[1,8,64]{2,0,1:T(1,128)S(1)}) all-reduce(f32[1,8,64]{2,0,1:T(1,128)S(1)} %get-tuple-element.53, f32[1,8,64]{2,0,1:T(1,128)S(1)} %get-tuple-element.54, f32[1,8,64]{2,0,1:T(1,128)S(1)} %get-tuple-element.52), channel_id=1, replica_groups=mesh['sensor'=128,'step'=4] {'sensor'}, use_global_device_ids=true, to_apply=%region_8.0 | all-reduce | flops 1536 | bytes 12288 | tf_op jit(solution)/shard_map/psum | solution.py:46
  519.7 1.3 fusion.34
  524.3 2.9 multiply_reduce_fusion.1
  527.2 2.3 copy.113
  529.5 2.1 reshape.91
  533.0 2.6 multiply_reduce_fusion.4
  536.3 2.0 subtract_divide_fusion
  538.3 2.1 reshape.92
  540.3 2.3 copy.114
  542.7 1.6 multiply_reduce_fusion
  544.9 2.3 fusion.30
  547.2 1.8 fusion.83
  549.1 2.6 fusion.16
  551.7 2.0 copy.123
  557.0 490.8 %all-reduce.3 = (f32[1,8,64]{2,0,1:T(1,128)S(1)}, f32[1,8,64]{2,0,1:T(1,128)S(1)}, f32[1,8,64]{2,0,1:T(1,128)S(1)}) all-reduce(f32[1,8,64]{2,0,1:T(1,128)S(1)} %get-tuple-element.50, f32[1,8,64]{2,0,1:T(1,128)S(1)} %get-tuple-element.51, f32[1,8,64]{2,0,1:T(1,128)S(1)} %get-tuple-element.49), channel_id=1, replica_groups=mesh['sensor'=128,'step'=4] {'sensor'}, use_global_device_ids=true, to_apply=%region_18.0 | all-reduce | flops 1536 | bytes 12288 | tf_op jit(solution)/shard_map/psum | solution.py:76
  1049.5 325.5 %all-reduce.14.cloned.1.call-done = (f32[1,8,64,64]{3,2,1,0:T(8,128)}, f32[1,8,64,64]{3,2,1,0:T(8,128)}, f32[1,8,64,64]{3,2,1,0:T(8,128)}) async-done(((f32[1,8,64,64]{3,2,1,0:T(8,128)}, f32[1,8,64,64]{3,2,1,0:T(8,128)}, f32[1,8,64,64]{3,2,1,0:T(8,128)}), (f32[1,8,64,64]{3,2,1,0:T(8,128)}, f32[1,8,64,64]{3,2,1,0:T(8,128)}, f32[1,8,64,64]{3,2,1,0:T(8,128)})) %all-reduce.14.cloned.1.call-update) | async-done | bytes 393232 | tf_op jit(solution)/shard_map/psum | solution.py:76
  1377.0 1.5 fusion.17
  1379.2 1.5 fusion.84
  1380.7 1.9 fusion.15
  1385.0 1.3 convolution_bitcast_fusion
  1391.4 346.1 %all-reduce.12.cloned.1.call-done = (f32[512,512]{0,1:T(8,128)}, f32[512,512]{0,1:T(8,128)}, f32[512,512]{0,1:T(8,128)}) async-done(((f32[512,512]{0,1:T(8,128)}, f32[512,512]{0,1:T(8,128)}, f32[512,512]{0,1:T(8,128)}), (f32[512,512]{0,1:T(8,128)}, f32[512,512]{0,1:T(8,128)}, f32[512,512]{0,1:T(8,128)})) %all-reduce.12.cloned.1.call-update) | async-done | bytes 3145744
  1737.5 1.8 constant_dynamic-slice_fusion.2
  1739.4 1.8 constant_dynamic-slice_fusion.1
  1741.2 1.8 constant_dynamic-slice_fusion
  1743.1 23.7 %reduce-scatter.7.cloned.1.call-done = f32[4,128]{0,1:T(8,128)} async-done(((f32[4,512]{0,1:T(8,128)}), f32[4,128]{0,1:T(8,128)}) %reduce-scatter.7.cloned.1.call-update) | async-done | bytes 2064 | tf_op jit(solution)/shard_map/reduce_scatter | solution.py:104
  1767.6 30.1 %reduce-scatter.9.cloned.1.call-done = f32[4,128]{0,1:T(8,128)} async-done(((f32[4,512]{0,1:T(8,128)}), f32[4,128]{0,1:T(8,128)}) %reduce-scatter.9.cloned.1.call-update) | async-done | bytes 2064 | tf_op jit(solution)/shard_map/reduce_scatter | solution.py:105
  1799.8 28.6 %reduce-scatter.11.cloned.1.call-done = f32[4,128]{0,1:T(8,128)} async-done(((f32[4,512]{0,1:T(8,128)}), f32[4,128]{0,1:T(8,128)}) %reduce-scatter.11.cloned.1.call-update) | async-done | bytes 2064 | tf_op jit(solution)/shard_map/reduce_scatter | solution.py:106
  (110 shorter events, 30.0 us)
Async XLA Ops:
  7.2 4.1 copy-start
  7.2 515.1 %all-reduce.16.cloned.1.call-start = ((), (), s32[]{:S(2)}) async-start(), calls=%async_computation.8 | async-start | bytes 1572864 | tf_op jit(solution)/shard_map/psum | solution.py:46
  7.9 1.3 copy-start.1
  9.2 1.4 copy-start.8
  16.1 1.0 copy-start.7
  16.1 1358.9 %all-reduce.14.cloned.1.call-start = ((), (), s32[]{:S(2)}) async-start(), calls=%async_computation.7 | async-start | bytes 1572864 | tf_op jit(solution)/shard_map/psum | solution.py:76
  519.7 1.3 copy-start.17
  521.1 1.0 copy-start.12
  522.3 1.0 copy-start.14
  523.4 1.0 copy-start.13
  524.3 2.9 copy-start.10
  535.6 0.7 copy-start.21
  544.3 0.6 copy-start.18
  544.9 2.3 copy-start.11
  544.9 2.3 copy-start.20
  547.2 1.8 copy-start.3
  553.7 1.3 copy-start.19
  554.9 1.1 copy-start.4
  1047.9 689.6 %all-reduce.12.cloned.1.call-start = ((), (), s32[]{:S(2)}) async-start(), calls=%async_computation.6 | async-start | bytes 6291456
  1375.0 1.0 copy-start.16
  1376.0 0.9 copy-start.15
  1377.0 1.5 copy-start.5
  1378.5 0.7 copy-start.22
  1379.2 1.5 copy-start.2
  1386.3 380.4 %reduce-scatter.7.cloned.1.call-start = ((), (), s32[]{:S(2)}) async-start(), calls=%async_computation.3 | async-start | bytes 327680 | tf_op jit(solution)/shard_map/reduce_scatter | solution.py:104
  1388.3 1.0 copy-start.6
  1389.3 1.0 copy-start.9
  1739.3 58.4 %reduce-scatter.9.cloned.1.call-start = ((), (), s32[]{:S(2)}) async-start(), calls=%async_computation.4 | async-start | bytes 327680 | tf_op jit(solution)/shard_map/reduce_scatter | solution.py:105
  1741.2 87.2 %reduce-scatter.11.cloned.1.call-start = ((), (), s32[]{:S(2)}) async-start(), calls=%async_computation.5 | async-start | bytes 327680 | tf_op jit(solution)/shard_map/reduce_scatter | solution.py:106
Sparse Core Ops, SparseCore 0:
  16.2 338.6 all-reduce.15
  1048.0 326.9 all-reduce.13
  1386.4 350.9 all-reduce.11
  1740.2 26.5 reduce-scatter.6
  1769.6 28.0 reduce-scatter.8
  1800.3 28.0 reduce-scatter.10
where the time goes:
time: 1840 us
  blocking collectives  989 us (54%)
  waiting for transfers between devices  754 us (41%)
  local copies, waits for them, and re-layouts  35.4 us (2%)
  matrix products  33.7 us (2%)
    psum x1, blocking collectives, shards(): lax.psum((local_summary[moment], local_normal[moment]), 'sensor')  498 us
    psum x1, blocking collectives, shards(): lax.psum((local_gsum[moment], local_gnorm[moment]), 'sensor')  491 us
    unnamed x7, waiting for transfers between devices  346 us
    psum x1, waiting for transfers between devices, shards(): lax.psum((local_gsum[moment], local_gnorm[moment]), 'sensor')  326 us
  transfers between devices with their start and end apart: 6, of which 5 were waited for; matrix products, arithmetic and copies ran while one was open for 1% of the time, Pallas kernels for 0%

commit v1 on v0

--- a/solution.py
+++ b/solution.py
@@ -1,11 +1,270 @@
+import functools
 import math
 
 import jax
 import jax.numpy as jnp
 from jax import lax
+from jax.experimental import pallas as pl
+from jax.experimental.pallas import tpu as pltpu
 from jax.sharding import PartitionSpec as P
 
+MESH = pl.DeviceIdType.MESH
+VM = pl.BlockSpec(memory_space=pltpu.VMEM)
+
+
+def place(grid):
+    _, zs, _ = grid
+    s = lax.axis_index("sensor")
+    return lax.axis_index("step"), s // (2 * zs), lax.rem(s // 2, zs), lax.rem(s, 2)
+
+
+def at(grid, x, y, z, c):
+    return ((y * grid[1] + z) * 2 + c, x)
+
+
+def send(src, dst, ssem, rsem, target):
+    copy = pltpu.make_async_remote_copy(
+        src_ref=src, dst_ref=dst, send_sem=ssem, recv_sem=rsem, device_id=target, device_id_type=MESH
+    )
+    return copy
+
+
+def greet(targets):
+    barrier = pltpu.get_barrier_semaphore()
+    for target in targets:
+        pl.semaphore_signal(barrier, inc=1, device_id=target, device_id_type=MESH)
+    pl.semaphore_wait(barrier, len(targets))
+
+
+def all_reduce_kernel(grid, x_ref, out_ref, buf_c, acc_c, buf_y, acc_y, buf_z, sc, rc, sy, ry, sz, rz):
+    ys, zs, _ = grid
+    tiles = x_ref.shape[2]
+    x, y, z, c = place(grid)
+    partner = at(grid, x, y, z, 1 - c)
+    y_peer = [at(grid, x, lax.rem(y + d, ys), z, c) for d in range(1, ys)]
+    z_peer = [at(grid, x, y, lax.rem(z + d, zs), c) for d in range(1, zs)]
+    greet([partner] + y_peer + z_peer)
+
+    pair = send(x_ref.at[1 - c], buf_c, sc.at[0], rc.at[0], partner)
+    pair.start()
+    pair.wait()
+    acc_c[...] = x_ref[c] + buf_c[...]
+
+    down = [
+        send(acc_c.at[lax.rem(y + d, ys)], buf_y.at[d - 1], sy.at[0, d - 1], ry.at[0, d - 1], y_peer[d - 1])
+        for d in range(1, ys)
+    ]
+    for copy in down:
+        copy.start()
+    for copy in down:
+        copy.wait()
+    acc_y[...] = acc_c[y] + sum(buf_y[d - 1] for d in range(1, ys))
+
+    for d in range(1, zs):
+        other = lax.rem(z + d, zs)
+
+        @pl.when(other < tiles)
+        def _():
+            send(acc_y.at[other], buf_z.at[d - 1], sz.at[0, d - 1], rz.at[0, d - 1], z_peer[d - 1]).start()
+
+    @pl.when(z < tiles)
+    def _():
+        for d in range(1, zs):
+            send(acc_y.at[0], buf_z.at[d - 1], sz.at[0, d - 1], rz.at[0, d - 1], z_peer[d - 1]).wait_recv()
+        out_ref[c, y, z] = acc_y[z] + sum(buf_z[d - 1] for d in range(1, zs))
+        for d in range(1, zs):
+            mine = out_ref.at[c, y, z]
+            send(mine, mine, sz.at[1, d - 1], rz.at[1, d - 1], z_peer[d - 1]).start()
+
+    for d in range(1, zs):
+        other = lax.rem(z + d, zs)
+
+        @pl.when(other < tiles)
+        def _():
+            send(acc_y.at[other], buf_z.at[d - 1], sz.at[0, d - 1], rz.at[0, d - 1], z_peer[d - 1]).wait_send()
+
+    for d in range(1, zs):
+        source = lax.rem(z + zs - d, zs)
+
+        @pl.when(source < tiles)
+        def _():
+            theirs = out_ref.at[c, y, source]
+            send(theirs, theirs, sz.at[1, d - 1], rz.at[1, d - 1], z_peer[d - 1]).wait_recv()
+
+    up = []
+    for d in range(1, ys):
+        mine = out_ref.at[c, y]
+        up.append(send(mine, mine, sy.at[1, d - 1], ry.at[1, d - 1], y_peer[d - 1]))
+    for copy in up:
+        copy.start()
+    for copy in up:
+        copy.wait()
+    mine = out_ref.at[c]
+    pair = send(mine, mine, sc.at[1], rc.at[1], partner)
+    pair.start()
+
+    @pl.when(z < tiles)
+    def _():
+        for d in range(1, zs):
+            mine = out_ref.at[c, y, z]
+            send(mine, mine, sz.at[1, d - 1], rz.at[1, d - 1], z_peer[d - 1]).wait_send()
+
+    pair.wait()
+
+
+def all_reduce(data, grid, ident):
+    ys, zs, _ = grid
+    _, _, tiles, rows, lanes = data.shape
+    dma = pltpu.SemaphoreType.DMA
+    block = (rows, lanes)
+    return pl.pallas_call(
+        functools.partial(all_reduce_kernel, grid),
+        out_shape=jax.ShapeDtypeStruct(data.shape, jnp.float32),
+        in_specs=[VM],
+        out_specs=VM,
+        scratch_shapes=[
+            pltpu.VMEM((ys, tiles) + block, jnp.float32),
+            pltpu.VMEM((ys, tiles) + block, jnp.float32),
+            pltpu.VMEM((ys - 1, tiles) + block, jnp.float32),
+            pltpu.VMEM((tiles,) + block, jnp.float32),
+            pltpu.VMEM((zs - 1,) + block, jnp.float32),
+            dma((2,)),
+            dma((2,)),
+            dma((2, ys - 1)),
+            dma((2, ys - 1)),
+            dma((2, zs - 1)),
+            dma((2, zs - 1)),
+        ],
+        compiler_params=pltpu.CompilerParams(collective_id=ident, has_side_effects=True, vmem_limit_bytes=32 << 20),
+    )(data)
+
+
+def scatter_kernel(
+    grid, scale, xf_ref, yf_ref, out_ref, xp, yp, xq, yq, xr, yr, xb, yb, xs, ys_, zsrc, zbuf,
+    s1, r1, s2, r2, s3, r3, sz, rz,
+):
+    ys, zs, xs_n = grid
+    x, y, z, c = place(grid)
+    partner = at(grid, x, y, z, 1 - c)
+    x_peer = [at(grid, lax.rem(x + d, xs_n), y, z, c) for d in range(1, xs_n)]
+    y_peer = [at(grid, x, lax.rem(y + d, ys), z, c) for d in range(1, ys)]
+    z_peer = [at(grid, x, y, lax.rem(z + d, zs), c) for d in range(1, zs)]
+    greet([partner] + x_peer + y_peer + z_peer)
+
+    first = [
+        send(xf_ref.at[1 - c], xp, s1.at[0], r1.at[0], partner),
+        send(yf_ref.at[1 - c], yp, s1.at[1], r1.at[1], partner),
+    ]
+    for copy in first:
+        copy.start()
+    first[0].wait()
+    xq[...] = xf_ref[c] + xp[...]
+    second_x = [
+        send(xq.at[lax.rem(x + d, xs_n)], xr.at[d - 1], s2.at[0, d - 1], r2.at[0, d - 1], x_peer[d - 1])
+        for d in range(1, xs_n)
+    ]
+    for copy in second_x:
+        copy.start()
+    first[1].wait()
+    yq[...] = yf_ref[c] + yp[...]
+    second_y = [
+        send(yq.at[lax.rem(y + d, ys)], yr.at[d - 1], s2.at[1, d - 1], r2.at[1, d - 1], y_peer[d - 1])
+        for d in range(1, ys)
+    ]
+    for copy in second_y:
+        copy.start()
+    for copy in second_x:
+        copy.wait()
+    xs[...] = xq[x] + sum(xr[d - 1] for d in range(1, xs_n))
+    third_y = [
+        send(xs.at[lax.rem(y + d, ys)], xb.at[d - 1], s3.at[0, d - 1], r3.at[0, d - 1], y_peer[d - 1])
+        for d in range(1, ys)
+    ]
+    for copy in third_y:
+        copy.start()
+    for copy in second_y:
+        copy.wait()
+    ys_[...] = yq[y] + sum(yr[d - 1] for d in range(1, ys))
+    third_x = [
+        send(ys_.at[lax.rem(x + d, xs_n)], yb.at[d - 1], s3.at[1, d - 1], r3.at[1, d - 1], x_peer[d - 1])
+        for d in range(1, xs_n)
+    ]
+    for copy in third_x:
+        copy.start()
+    for copy in third_y:
+        copy.wait()
+    half = zs // 2
+    weights = xs.shape[1]
+    low = xs[y] + sum(xb[d - 1] for d in range(1, ys))
+    for w in range(weights):
+        zsrc[0:half, w] = low[w].reshape(half, 4, 128)
+    for copy in third_x:
+        copy.wait()
+    high = ys_[x] + sum(yb[d - 1] for d in range(1, xs_n))
+    for w in range(weights):
+        zsrc[half:zs, w] = high[w].reshape(half, 4, 128)
+    last = [
+        send(zsrc.at[lax.rem(z + d, zs)], zbuf.at[d - 1], sz.at[d - 1], rz.at[d - 1], z_peer[d - 1])
+        for d in range(1, zs)
+    ]
+    for copy in last:
+        copy.start()
+    for copy in last:
+        copy.wait()
+    out_ref[...] = (zsrc[z] + sum(zbuf[d - 1] for d in range(1, zs))) * scale
+
+
+def scatter_sum(x_first, y_first, grid, scale, ident):
+    ys, zs, xs = grid
+    weights, rows, lanes = x_first.shape[3:]
+    dma = pltpu.SemaphoreType.DMA
+    block = (weights, rows, lanes)
+    f32 = jnp.float32
+    return pl.pallas_call(
+        functools.partial(scatter_kernel, grid, scale),
+        out_shape=jax.ShapeDtypeStruct((weights, 4, lanes), f32),
+        in_specs=[VM, VM],
+        out_specs=VM,
+        scratch_shapes=[
+            pltpu.VMEM((xs, ys) + block, f32),
+            pltpu.VMEM((ys, xs) + block, f32),
+            pltpu.VMEM((xs, ys) + block, f32),
+            pltpu.VMEM((ys, xs) + block, f32),
+            pltpu.VMEM((xs - 1, ys) + block, f32),
+            pltpu.VMEM((ys - 1, xs) + block, f32),
+            pltpu.VMEM((ys - 1,) + block, f32),
+            pltpu.VMEM((xs - 1,) + block, f32),
+            pltpu.VMEM((ys,) + block, f32),
+            pltpu.VMEM((xs,) + block, f32),
+            pltpu.VMEM((zs, weights, 4, lanes), f32),
+            pltpu.VMEM((zs - 1, weights, 4, lanes), f32),
+            dma((2,)),
+            dma((2,)),
+            dma((2, max(xs, ys) - 1)),
+            dma((2, max(xs, ys) - 1)),
+            dma((2, max(xs, ys) - 1)),
+            dma((2, max(xs, ys) - 1)),
+            dma((zs - 1,)),
+            dma((zs - 1,)),
+        ],
+        compiler_params=pltpu.CompilerParams(collective_id=ident, has_side_effects=True, vmem_limit_bytes=48 << 20),
+    )(x_first, y_first)
+
 HIGH = lax.Precision.HIGHEST
+YS, ZS, XS = 4, 16, 4
+GRID = (YS, ZS, XS)
+
+
+def sum_over_sensors(summary, normal, ident):
+    steps, heads, feats, width = summary.shape
+    tiles = summary.reshape(steps, heads // 2, 2, feats, width).transpose(0, 1, 3, 2, 4)
+    tiles = tiles.reshape(2, YS, 12, 8, 128)
+    extra = jnp.pad(normal.reshape(12, 128), ((0, 4), (0, 0))).reshape(2, YS, 1, 2, 128)
+    extra = jnp.pad(extra, ((0, 0), (0, 0), (0, 0), (0, 6), (0, 0)))
+    total = all_reduce(jnp.concatenate((tiles, extra), 2), GRID, ident)
+    summed = total[:, :, :12].reshape(steps, heads // 2, feats, 2, width).transpose(0, 1, 3, 2, 4)
+    normal_sum = total[:, :, 12, :2].reshape(16, 128)[:12]
+    return summed.reshape(summary.shape), normal_sum.reshape(normal.shape)
 
 
 def feature_map(scaled, feature_proj):
@@ -42,12 +301,7 @@
     masked_key = feat_key * valid[None, :, None, None]
     local_summary = jnp.einsum("tnhr,tnhe->thre", masked_key, values, precision=HIGH)
     local_normal = jnp.sum(masked_key, 1)
-    summed = [
-        lax.psum((local_summary[moment], local_normal[moment]), "sensor")
-        for moment in range(steps_here)
-    ]
-    summary = jnp.stack([entry[0] for entry in summed])
-    normal_sum = jnp.stack([entry[1] for entry in summed])
+    summary, normal_sum = sum_over_sensors(local_summary, local_normal, 0)
     numer = jnp.einsum("tnhr,thre->tnhe", feat_query, summary, precision=HIGH)
     denom = jnp.einsum("tnhr,thr->tnh", feat_query, normal_sum, precision=HIGH)
     attended = numer / denom[..., None]
@@ -72,12 +326,7 @@
     )
     local_gsum = jnp.einsum("tnhr,tnhe->thre", feat_query, grad_num, precision=HIGH)
     local_gnorm = jnp.einsum("tnhr,tnh->thr", feat_query, grad_den, precision=HIGH)
-    gathered = [
-        lax.psum((local_gsum[moment], local_gnorm[moment]), "sensor")
-        for moment in range(steps_here)
-    ]
-    grad_summary = jnp.stack([entry[0] for entry in gathered])
-    grad_normal = jnp.stack([entry[1] for entry in gathered])
+    grad_summary, grad_normal = sum_over_sensors(local_gsum, local_gnorm, 1)
     grad_fk = (
         jnp.einsum("tnhe,thre->tnhr", values, grad_summary, precision=HIGH) + grad_normal[:, None]
     ) * valid[None, :, None, None]
@@ -95,19 +344,13 @@
     weight_q = jnp.einsum("nd,nk->dk", flat_in, grad_q, preferred_element_type=jnp.float32)
     weight_k = jnp.einsum("nd,nk->dk", flat_in, grad_k, preferred_element_type=jnp.float32)
     weight_v = jnp.einsum("nd,nk->dk", flat_in, grad_val, preferred_element_type=jnp.float32)
-    partial_sums = (
-        lax.psum_scatter(weight_q, "sensor", scatter_dimension=0, tiled=True),
-        lax.psum_scatter(weight_k, "sensor", scatter_dimension=0, tiled=True),
-        lax.psum_scatter(weight_v, "sensor", scatter_dimension=0, tiled=True),
-    )
-    reduced = (
-        lax.psum_scatter(partial_sums[0], "step", scatter_dimension=1, tiled=True),
-        lax.psum_scatter(partial_sums[1], "step", scatter_dimension=1, tiled=True),
-        lax.psum_scatter(partial_sums[2], "step", scatter_dimension=1, tiled=True),
-    )
     total_rows = steps_here * lax.axis_size("step") * sensors_here * lax.axis_size("sensor")
     norm_scale = 1.0 / math.sqrt(total_rows)
-    return (grad_inputs, reduced[0] * norm_scale, reduced[1] * norm_scale, reduced[2] * norm_scale)
+    stacked = jnp.stack((weight_q, weight_k, weight_v)).reshape(3, YS, 2, ZS // 2, 2, 4, XS, 128)
+    x_first = stacked[:, :, 0].transpose(3, 5, 1, 0, 2, 4, 6).reshape(2, XS, YS, 3, ZS * 2, 128)
+    y_first = stacked[:, :, 1].transpose(3, 1, 5, 0, 2, 4, 6).reshape(2, YS, XS, 3, ZS * 2, 128)
+    reduced = scatter_sum(x_first, y_first, GRID, norm_scale, 2)
+    return (grad_inputs, reduced[0], reduced[1], reduced[2])
 
 
 def solution(mesh):

time: 1840 us -> 194 us (0.11)
  blocking collectives: 989 us -> 0 us
  waiting for transfers between devices: 754 us -> 0 us
  Pallas kernels: 0 us -> 112 us
    psum x2 -> x0, blocking collectives: 989 us -> none  [the longest x1 498 us: shards(): lax.psum((local_summary[moment], local_normal[moment]), 'sensor')]
    unnamed x7 -> x0, waiting for transfers between devices: 346 us -> none
    psum x2 -> x0, waiting for transfers between devices: 326 us -> none  [the longest x1 326 us: shards(): lax.psum((local_gsum[moment], local_gnorm[moment]), 'sensor')]
    pallas_call x0 -> x3, Pallas kernels: none -> 112 us  [the longest x2 77.5 us: all_reduce(): pl.pallas_call(functools.partial(all_reduce_kernel, grid), out_shape=jax....]
    reduce_scatter x3 -> x0, waiting for transfers between devices: 82.3 us -> none  [the longest x1 30.1 us: shards(): lax.psum_scatter(partial_sums[1], 'step', scatter_dimension=1, tiled=True)]
  transfers between devices with their start and end apart: 6 -> 0, of which waited for: 5 -> 0; matrix products, arithmetic and copies ran while one was open for 1% -> 0% of each run, Pallas kernels for 0% -> 0%
where the time goes in v1:
time: 194 us; the launch traced here: 192 us
  Pallas kernels  112 us (58%)
  local copies, waits for them, and re-layouts  37.9 us (20%)
  matrix products  36.9 us (19%)
  other arithmetic  3.61 us (2%)
    pallas_call x2, Pallas kernels, all_reduce(): pl.pallas_call(functools.partial(all_reduce_kernel, grid), out_shape=jax....  77.5 us
    pallas_call x1, Pallas kernels, scatter_sum(): pl.pallas_call(functools.partial(scatter_kernel, grid, scale), out_shape=...  34.5 us
    another operation x4, local copies, waits for them, and re-layouts, shards(): jnp.stack((weight_q, weight_k, weight_v))  5.76 us
    dot_general x2, matrix products, feature_back(): jnp.einsum('...hr,her->...he', weighted, feature_proj, precision=HIGH)  5.26 us
    dot_general x3, matrix products, project(): jnp.dot(flat_in, weight, preferred_element_type=jnp.float32)  5.02 us
    unnamed x35, local copies, waits for them, and re-layouts  4.86 us
    dot_general x2, matrix products, feature_map(): jnp.einsum('...he,her->...hr', scaled, feature_proj, precision=HIGH)  3.97 us

profile of v1, /device:TPU:1, one launch (start us, length us, event | category | flops | bytes accessed | tf_op | source)
XLA Modules:
  0.0 192.2 jit_solution(8808691657548189887)
XLA Ops:
  0.7 1.3 copy.175
  2.0 2.3 %multiply_reduce_fusion.2 = (f32[3,64,8]{1,2,0:T(8,128)S(1)}, f32[3,64,8,64]{1,3,2,0:T(8,128)S(1)}, f32[3,64,8,64]{1,3,2,0:T(8,128)}) fusion(bf16[8,64,512,1]{2,1,0,3:T(8,128)(2,1)S(1)} %bitcast.207, bf16[3,64,512]{2,1,0:T(8,128)(2,1)} %param.9), kind=kOutput, calls=%fused_computation.44 | convolution fusion | flops 100956672 | bytes 1513472 | tf_op jit(solution)/shard_map/dot_general | solution.py:292
  4.3 1.5 fusion.4
  6.8 1.3 multiply_reduce_fusion.3
  8.1 2.5 %fusion.72 = (f32[3,8,64]{2,0,1:T(4,128)S(1)}, f32[3,64,8,64]{3,1,0,2:T(8,128)S(1)}, f32[3,64,8,64]{3,1,0,2:T(8,128)}) fusion(f32[64]{0:T(128)S(1)} %compare_select_fusion, f32[3,64,8]{1,0,2:T(4,128)S(1)} %copy.169, f32[8,64,64]{2,1,0:T(8,128)S(1)} %copy-done, f32[3,64,8,64]{1,3,2,0:T(8,128)S(1)} %get-tuple-element.11), kind=kOutput, calls=%fused_computation.117 | convolution fusion | flops 75790848 | bytes 1323264 | tf_op jit(solution)/shard_map/...he,her->...hr/dot_general | solution.py:271
  11.7 1.4 fusion.48
  13.1 1.4 fusion.26
  14.5 1.5 copy.282
  16.0 1.6 reshape.143
  17.7 46.8 %shard_map.120 = f32[2,4,13,8,128]{4,3,2,1,0:T(8,128)S(1)} custom-call(f32[2,4,13,8,128]{4,3,2,1,0:T(8,128)S(1)} %select_maximum_fusion.1.x_ref), custom_call_target="tpu_custom_call" | custom-call | tf_op jit(solution)/shard_map/pallas_call | solution.py:120
  64.7 1.3 fusion.32
  67.1 2.3 %multiply_reduce_fusion.1 = (f32[3,64]{1,0:T(4,128)S(1)}, f32[3,64,8,64]{1,3,2,0:T(8,128)}) fusion(f32[3,64,8]{1,2,0:T(8,128)S(1)} %bitcast.212, f32[3,8,64,64]{2,3,1,0:T(8,128)S(1)} %bitcast.209, f32[3,64,8,64]{3,1,0,2:T(8,128)S(1)} %fusion.4), kind=kOutput, calls=%fused_computation.43 | convolution fusion | flops 75792192 | bytes 1186560 | tf_op jit(solution)/shard_map/tnhr,thre->tnhe/dot_general | solution.py:305
  69.4 1.4 copy.181
  72.9 1.9 fusion.77
  74.8 2.0 %multiply_reduce_fusion.4 = (f32[192]{0:T(256)S(1)}, f32[192,512]{1,0:T(8,128)S(1)}) fusion(f32[192,512]{1,0:T(8,128)} %reshape.150, f32[192]{0:T(256)S(1)} %sqrt.12, bf16[512,256]{1,0:T(8,128)(2,1)} %param.14, f32[192,256]{1,0:T(8,128)} %fusion.77), kind=kOutput, calls=%fused_computation.60 | convolution fusion | flops 102137664 | bytes 1246720 | tf_op jit(solution)/shard_map/dot_general | solution.py:318
  80.0 1.6 multiply_reduce_fusion
  82.8 3.0 %fusion.75 = (f32[3,64,8]{1,0,2:T(4,128)S(1)}, f32[3,64,8,64]{3,1,0,2:T(8,128)S(1)}) fusion(f32[3,64,8,64]{3,1,0,2:T(8,128)S(1)} %fusion.4, f32[3,8,64]{2,0,1:T(4,128)S(1)} %copy.188, f32[3,64,8]{1,0,2:T(4,128)S(1)} %copy.187, f32[3,8,64,64]{2,3,0,1:T(8,128)} %bitcast.201, f32[3,64,8,64]{1,3,2,0:T(8,128)S(1)} %get-tuple-element.9), kind=kOutput, calls=%fused_computation.118 | convolution fusion | flops 75889152 | bytes 1591296 | tf_op jit(solution)/shard_map/tnhe,thre->tnhr/dot_general | solution.py:324
  85.8 2.6 %fusion.16 = bf16[3,64,8,64]{1,3,2,0:T(8,128)(2,1)} fusion(f32[3,64,8,64]{3,1,0,2:T(8,128)S(1)} %get-tuple-element.25, f32[3,64,8,64]{1,3,2,0:T(8,128)S(1)} %copy-done.6, f32[3,64,8]{1,2,0:T(8,128)S(1)} %copy_multiply_fusion.1, f32[8,64,64]{2,1,0:T(8,128)S(1)} %copy-done), kind=kOutput, calls=%fused_computation.28 | convolution fusion | flops 75890688 | bytes 1120256 | tf_op jit(solution)/shard_map/...hr,her->...he/dot_general | solution.py:279
  88.5 2.0 %copy.192 = bf16[3,64,8,64]{3,2,1,0:T(8,128)(2,1)} copy(bf16[3,64,8,64]{1,3,2,0:T(8,128)(2,1)} %fusion.16) | data formatting | bytes 393216 | tf_op jit(solution)/shard_map/convert_element_type | solution.py:337
  93.7 1.4 fusion.28
  96.2 30.7 %shard_map.121 = f32[2,4,13,8,128]{4,3,2,1,0:T(8,128)S(1)} custom-call(f32[2,4,13,8,128]{4,3,2,1,0:T(8,128)S(1)} %select_maximum_fusion.x_ref), custom_call_target="tpu_custom_call" | custom-call | tf_op jit(solution)/shard_map/pallas_call | solution.py:120
  127.8 1.5 reshape.156
  129.4 2.6 %fusion.76 = (f32[3,64,8]{1,0,2:T(4,128)S(1)}, f32[3,64,8,64]{3,1,0,2:T(8,128)S(1)}) fusion(f32[3,64,8,64]{3,1,0,2:T(8,128)} %get-tuple-element.19, f32[64]{0:T(128)S(1)} %get-tuple-element.28, f32[3,8,64]{2,0,1:T(4,128)S(1)} %copy.197, f32[3,8,64,64]{3,2,0,1:T(8,128)S(1)} %bitcast.202, f32[3,64,8,64]{3,1,2,0:T(8,128)S(1)} %copy-done.2), kind=kOutput, calls=%fused_computation.119 | convolution fusion | flops 75987456 | bytes 1585408 | tf_op jit(solution)/shard_map/tnhe,thre->tnhr/dot_general | solution.py:331
  132.1 2.6 %fusion.15 = bf16[3,64,8,64]{1,3,2,0:T(8,128)(2,1)} fusion(f32[3,64,8,64]{3,1,0,2:T(8,128)S(1)} %get-tuple-element.27, f32[3,64,8,64]{1,3,2,0:T(8,128)S(1)} %copy-done.5, f32[3,64,8]{1,2,0:T(8,128)S(1)} %copy_multiply_fusion, f32[8,64,64]{2,1,0:T(8,128)S(1)} %copy-done), kind=kOutput, calls=%fused_computation.27 | convolution fusion | flops 75890688 | bytes 1120256 | tf_op jit(solution)/shard_map/...hr,her->...he/dot_general | solution.py:279
  136.3 1.4 convolution_add_fusion.2
  137.8 1.4 fusion.17
  142.4 1.6 stack.12
  146.7 1.6 stack.13
  149.8 1.3 copy.208
  151.1 1.6 stack.14
  153.7 2.6 %slice_bitcast_fusion = (f32[2,4,4,3,8,4,128]{6,2,5,0,4,1,3:T(4,128)S(1)}, f32[2,4,4,3,8,4,128]{6,1,5,0,4,2,3:T(4,128)S(1)}) fusion(f32[3,4,2,8,2,4,4,128]{7,6,5,4,3,2,1,0:T(4,128)} %constant_dynamic-update-slice_fusion), kind=kLoop, calls=%fused_computation | loop fusion | bytes 6291456 | tf_op jit(solution)/shard_map/transpose | solution.py:351
  157.1 34.5 %shard_map.122 = f32[3,4,128]{2,1,0:T(4,128)S(1)} custom-call(f32[2,4,4,3,32,128]{5,4,3,2,1,0:T(8,128)S(1)} %bitcast.190, f32[2,4,4,3,32,128]{5,4,3,2,1,0:T(8,128)S(1)} %bitcast.191), custom_call_target="tpu_custom_call" | custom-call | tf_op jit(solution)/shard_map/pallas_call | solution.py:223
  (92 shorter events, 25.9 us)
Async XLA Ops:
  0.6 3.7 %copy-start = (f32[8,64,64]{2,1,0:T(8,128)S(1)}, f32[8,64,64]{2,1,0:T(8,128)}, u32[]{:S(2)}) copy-start(f32[8,64,64]{2,1,0:T(8,128)} %param.16) | copy-start | bytes 393220
  0.6 6.1 %copy-start.3 = (bf16[3,64,512]{2,1,0:T(8,128)(2,1)S(1)}, bf16[3,64,512]{2,1,0:T(8,128)(2,1)}, u32[]{:S(2)}) copy-start(bf16[3,64,512]{2,1,0:T(8,128)(2,1)} %param.9) | copy-start | bytes 589828
  0.7 5.9 %copy-start.7 = (bf16[512,512]{1,0:T(8,128)(2,1)S(1)}, bf16[512,512]{1,0:T(8,128)(2,1)}, u32[]{:S(2)}) copy-start(bf16[512,512]{1,0:T(8,128)(2,1)} %param.12) | copy-start | bytes 1572868
  5.8 4.9 %copy-start.10 = (bf16[512,512]{1,0:T(8,128)(2,1)S(1)}, bf16[512,512]{1,0:T(8,128)(2,1)}, u32[]{:S(2)}) copy-start(bf16[512,512]{1,0:T(8,128)(2,1)} %param.13) | copy-start | bytes 1572868
  13.1 51.4 %copy-start.1 = (f32[3,64,8,64]{3,1,2,0:T(8,128)}, f32[3,64,8,64]{3,1,2,0:T(8,128)S(1)}, u32[]{:S(2)}) copy-start(f32[3,64,8,64]{3,1,2,0:T(8,128)S(1)} %fusion.48) | copy-start | bytes 1179652
  71.8 5.0 %copy-start.14 = (f32[192,512]{1,0:T(8,128)S(1)}, f32[192,512]{1,0:T(8,128)}, u32[]{:S(2)}) copy-start(f32[192,512]{1,0:T(8,128)} %reshape.150) | copy-start | bytes 1179652
  82.8 3.0 %copy-start.6 = (f32[3,64,8,64]{1,3,2,0:T(8,128)S(1)}, f32[3,64,8,64]{1,3,2,0:T(8,128)}, u32[]{:S(2)}) copy-start(f32[3,64,8,64]{1,3,2,0:T(8,128)} %get-tuple-element.17) | copy-start | bytes 1179652
  82.8 8.9 %copy-start.9 = (bf16[512,512]{1,0:T(8,128)(2,1)S(1)}, bf16[512,512]{1,0:T(8,128)(2,1)}, u32[]{:S(2)}) copy-start(bf16[512,512]{1,0:T(8,128)(2,1)} %param.11) | copy-start | bytes 1572868
  91.7 3.4 %copy-start.12 = (bf16[192,512]{1,0:T(8,128)(2,1)}, bf16[192,512]{1,0:T(8,128)(2,1)S(1)}, u32[]{:S(2)}) copy-start(bf16[192,512]{1,0:T(8,128)(2,1)S(1)} %convert_element_type.63) | copy-start | bytes 589828
  95.7 33.7 %copy-start.2 = (f32[3,64,8,64]{3,1,2,0:T(8,128)S(1)}, f32[3,64,8,64]{3,1,2,0:T(8,128)}, u32[]{:S(2)}) copy-start(f32[3,64,8,64]{3,1,2,0:T(8,128)} %copy-done.1) | copy-start | bytes 1179652
  127.8 4.3 %copy-start.5 = (f32[3,64,8,64]{1,3,2,0:T(8,128)S(1)}, f32[3,64,8,64]{1,3,2,0:T(8,128)}, u32[]{:S(2)}) copy-start(f32[3,64,8,64]{1,3,2,0:T(8,128)} %get-tuple-element.18) | copy-start | bytes 1179652
  132.1 4.2 %copy-start.8 = (bf16[512,512]{1,0:T(8,128)(2,1)S(1)}, bf16[512,512]{1,0:T(8,128)(2,1)}, u32[]{:S(2)}) copy-start(bf16[512,512]{1,0:T(8,128)(2,1)} %param.12) | copy-start | bytes 1572868
  136.3 3.5 %copy-start.11 = (bf16[512,512]{1,0:T(8,128)(2,1)S(1)}, bf16[512,512]{1,0:T(8,128)(2,1)}, u32[]{:S(2)}) copy-start(bf16[512,512]{1,0:T(8,128)(2,1)} %param.13) | copy-start | bytes 1572868
  137.7 3.1 %copy-start.4 = (bf16[3,64,512]{2,1,0:T(8,128)(2,1)S(1)}, bf16[3,64,512]{2,1,0:T(8,128)(2,1)}, u32[]{:S(2)}) copy-start(bf16[3,64,512]{2,1,0:T(8,128)(2,1)} %param.9) | copy-start | bytes 589828
  137.7 3.1 %copy-start.13 = (bf16[192,512]{1,0:T(8,128)(2,1)S(1)}, bf16[192,512]{1,0:T(8,128)(2,1)}, u32[]{:S(2)}) copy-start(bf16[192,512]{1,0:T(8,128)(2,1)} %copy-done.12) | copy-start | bytes 589828

commit v2 on v0

v2 whole, which is shorter than its diff:
```python
import functools
import math

import jax
import jax.numpy as jnp
from jax import lax
from jax.experimental import pallas as pl
from jax.experimental.pallas import tpu as pltpu
from jax.sharding import PartitionSpec as P

MESH = pl.DeviceIdType.MESH
VM = pl.BlockSpec(memory_space=pltpu.VMEM)
SM = pl.BlockSpec(memory_space=pltpu.SMEM)
F32, BF16 = jnp.float32, jnp.bfloat16
YS, ZS, XS = 4, 16, 4
T, N, D, F, H, E = 3, 64, 512, 256, 8, 64
ROWS = T * N
PAIRS = H // 2
TILES = 13
QUAD = 256
FACTOR = E ** (-0.25)


def at(x, y, z, c):
    return ((y * ZS + z) * 2 + c, x)


def send(src, dst, ssem, rsem, target):
    return pltpu.make_async_remote_copy(
        src_ref=src, dst_ref=dst, send_sem=ssem, recv_sem=rsem, device_id=target, device_id_type=MESH
    )


def start(copies):
    for copy in copies:
        copy.start()


def wait(copies):
    for copy in copies:
        copy.wait()


def dot(a, b):
    return lax.dot_general(a, b, (((1,), (0,)), ((), ())), preferred_element_type=F32)


def dot_nt(a, b):
    return lax.dot_general(a, b, (((1,), (1,)), ((), ())), preferred_element_type=F32)


def dot_tn(a, b):
    return lax.dot_general(a, b, (((0,), (0,)), ((), ())), preferred_element_type=F32)


def split(value):
    high = value.astype(BF16)
    return high, (value - high.astype(F32)).astype(BF16)


def dot3(product, a, b):
    return product(a[0], b[0]) + product(a[1], b[0]) + product(a[0], b[1])


def head_sum(value, ones):
    high, low = split(value)
    return dot(high, ones) + dot(low, ones)


def gelu_slope(v):
    k = math.sqrt(2 / math.pi)
    th = jnp.tanh(k * (v + 0.044715 * v * v * v))
    return 0.5 * (1.0 + th) + 0.5 * v * (1.0 - th * th) * (k * (1.0 + 3 * 0.044715 * v * v))


class Reduce:
    def __init__(self, pos, peers, r, tag):
        self.pos, self.peers = pos, peers
        self.x, self.out = r["x" + tag], r["out" + tag]
        self.buf_c, self.acc_c = r["bufc" + tag], r["accc" + tag]
        self.buf_y, self.acc_y, self.buf_z = r["bufy" + tag], r["accy" + tag], r["bufz" + tag]
        self.sc, self.rc, self.sy, self.ry = r["sc" + tag], r["rc" + tag], r["sy" + tag], r["ry" + tag]
        self.sz, self.rz = r["sz" + tag], r["rz" + tag]

    def start_core(self):
        c = self.pos[3]
        self.core = send(self.x.at[1 - c], self.buf_c, self.sc.at[0], self.rc.at[0], self.peers["c"])
        self.core.start()

    def start_y(self):
        _, y, _, c = self.pos
        self.core.wait()
        self.acc_c[...] = self.x[c] + self.buf_c[...]
        self.down = [
            send(
                self.acc_c.at[lax.rem(y + d, YS)], self.buf_y.at[d - 1], self.sy.at[0, d - 1], self.ry.at[0, d - 1],
                self.peers["y"][d - 1],
            )
            for d in range(1, YS)
        ]
        start(self.down)

    def z_down(self, d, slot):
        return send(
            self.acc_y.at[slot], self.buf_z.at[d - 1], self.sz.at[0, d - 1], self.rz.at[0, d - 1], self.peers["z"][d - 1]
        )

    def z_up(self, d, slot):
        piece = self.out.at[self.pos[3], self.pos[1], slot]
        return send(piece, piece, self.sz.at[1, d - 1], self.rz.at[1, d - 1], self.peers["z"][d - 1])

    def start_z(self):
        _, y, z, _ = self.pos
        wait(self.down)
        self.acc_y[...] = self.acc_c[y] + self.buf_y[0] + self.buf_y[1] + self.buf_y[2]
        for d in range(1, ZS):
            other = lax.rem(z + d, ZS)

            @pl.when(other < TILES)
            def _():
                self.z_down(d, other).start()

    def start_z_back(self):
        _, y, z, c = self.pos

        @pl.when(z < TILES)
        def _():
            for d in range(1, ZS):
                self.z_down(d, 0).wait_recv()
            self.out[c, y, z] = self.acc_y[z] + sum(self.buf_z[d - 1] for d in range(1, ZS))
            for d in range(1, ZS):
                self.z_up(d, z).start()

    def start_y_back(self):
        _, y, z, c = self.pos
        for d in range(1, ZS):
            source = lax.rem(z + ZS - d, ZS)

            @pl.when(source < TILES)
            def _():
                self.z_up(d, source).wait_recv()

        mine = self.out.at[c, y]
        self.up = [
            send(mine, mine, self.sy.at[1, d - 1], self.ry.at[1, d - 1], self.peers["y"][d - 1]) for d in range(1, YS)
        ]
        start(self.up)

    def start_core_back(self):
        c = self.pos[3]
        wait(self.up)
        mine = self.out.at[c]
        self.core = send(mine, mine, self.sc.at[1], self.rc.at[1], self.peers["c"])
        self.core.start()

    def finish(self):
        self.core.wait()

    def drain(self):
        z = self.pos[2]
        for d in range(1, ZS):
            other = lax.rem(z + d, ZS)

            @pl.when(other < TILES)
            def _():
                self.z_down(d, other).wait_send()

        @pl.when(z < TILES)
        def _():
            for d in range(1, ZS):
                self.z_up(d, z).wait_send()


def tile_place(tile):
    group, slot = divmod(tile, 12)
    return group // YS, group % YS, slot


def put_blocks(ref, moment, quad, result):
    first = lax.broadcasted_iota(jnp.int32, (E, 128), 1) < E
    for j in range(2):
        part = result[128 * j : 128 * j + 128, 128 * j : 128 * j + 128]
        block = jnp.where(first, part[0:E], part[E:128]).reshape(8, 8, 128)
        for half in range(2):
            c, y, slot = tile_place((moment * PAIRS + 2 * quad + j) * 8 + 4 * half)
            ref[c, y, pl.ds(slot, 4)] = block[4 * half : 4 * half + 4]


def row_place(moment, pair):
    row = moment * PAIRS + pair
    group = row // 2
    return group // YS, group % YS, row % 2


def put_row(ref, moment, pair, row):
    c, y, k = row_place(moment, pair)
    ref[c, y, TILES - 1, pl.ds(k, 1)] = row


def get_row(ref, moment, quad):
    rows = []
    for j in range(2):
        c, y, k = row_place(moment, 2 * quad + j)
        rows.append(ref[c, y, TILES - 1, pl.ds(k, 1)])
    return jnp.concatenate(rows, axis=1)


def get_blocks(ref, moment, quad, high_ref, low_ref):
    first = lax.broadcasted_iota(jnp.int32, (E, 128), 1) < E
    for j in range(2):
        halves = []
        for half in range(2):
            c, y, slot = tile_place((moment * PAIRS + 2 * quad + j) * 8 + 4 * half)
            halves.append(ref[c, y, pl.ds(slot, 4)].reshape(32, 128))
        block = jnp.concatenate(halves, axis=0)
        for k, kept in enumerate((jnp.where(first, block, 0.0), jnp.where(first, 0.0, block))):
            high, low = split(kept)
            here = pl.ds(128 * j + E * k, E), pl.ds(128 * j, 128)
            high_ref[moment, quad, here[0], here[1]] = high
            low_ref[moment, quad, here[0], here[1]] = low


class Scatter:
    def __init__(self, pos, peers, r, tag, count):
        self.pos, self.peers, self.count, self.r, self.tag = pos, peers, count, r, tag

    def ref(self, name):
        return self.r[name + self.tag]

    def put(self, name, index, result):
        xf, yf = self.ref(name + "x"), self.ref(name + "y")
        for y in range(YS):
            for x in range(XS):
                block = result[64 * y : 64 * y + 64, 128 * x : 128 * x + 128]
                xf[index, x, y] = block[0:32]
                yf[index, y, x] = block[32:64]

    def core_copies(self, index):
        s, q = self.ref("s1"), self.ref("r1")
        return [
            send(self.ref("sendx").at[index], self.ref("gotx").at[index], s.at[0, index], q.at[0, index], self.peers["c"]),
            send(self.ref("sendy").at[index], self.ref("goty").at[index], s.at[1, index], q.at[1, index], self.peers["c"]),
        ]

    def second_copies(self, index):
        x, y, _, _ = self.pos
        s, q = self.ref("s2"), self.ref("r2")
        copies = []
        for d in range(1, XS):
            copies.append(
                send(
                    self.ref("ownx").at[index, lax.rem(x + d, XS)], self.ref("bx").at[index, d - 1],
                    s.at[0, index, d - 1], q.at[0, index, d - 1], self.peers["x"][d - 1],
                )
            )
            copies.append(
                send(
                    self.ref("owny").at[index, lax.rem(y + d, YS)], self.ref("by").at[index, d - 1],
                    s.at[1, index, d - 1], q.at[1, index, d - 1], self.peers["y"][d - 1],
                )
            )
        return copies

    def start_second(self, index):
        wait(self.core_copies(index))
        for name in ("x", "y"):
            own, got = self.ref("own" + name), self.ref("got" + name)
            own[index] = own[index] + got[index]
        start(self.second_copies(index))

    def third_copies(self, index):
        x, y, _, _ = self.pos
        s, q = self.ref("s3"), self.ref("r3")
        copies = []
        for d in range(1, XS):
            copies.append(
                send(
                    self.ref("cx").at[index, lax.rem(y + d, YS)], self.ref("dx").at[index, d - 1],
                    s.at[0, index, d - 1], q.at[0, index, d - 1], self.peers["y"][d - 1],
                )
            )
            copies.append(
                send(
                    self.ref("cy").at[index, lax.rem(x + d, XS)], self.ref("dy").at[index, d - 1],
                    s.at[1, index, d - 1], q.at[1, index, d - 1], self.peers["x"][d - 1],
                )
            )
        return copies

    def start_third(self, index):
        x, y, _, _ = self.pos
        wait(self.second_copies(index))
        bx, by = self.ref("bx"), self.ref("by")
        self.ref("cx")[index] = self.ref("ownx")[index, x] + bx[index, 0] + bx[index, 1] + bx[index, 2]
        self.ref("cy")[index] = self.ref("owny")[index, y] + by[index, 0] + by[index, 1] + by[index, 2]
        start(self.third_copies(index))

    def last_copies(self):
        z = self.pos[2]
        return [
            send(
                self.ref("zs").at[lax.rem(z + d, ZS)], self.ref("zb").at[d - 1],
                self.ref("s4").at[d - 1], self.ref("r4").at[d - 1], self.peers["z"][d - 1],
            )
            for d in range(1, ZS)
        ]

    def start_last(self):
        x, y, _, _ = self.pos
        zs = self.ref("zs")
        for index in range(self.count):
            wait(self.third_copies(index))
            dx, dy = self.ref("dx"), self.ref("dy")
            low = self.ref("cx")[index, y] + dx[index, 0] + dx[index, 1] + dx[index, 2]
            high = self.ref("cy")[index, x] + dy[index, 0] + dy[index, 1] + dy[index, 2]
            zs[0:8, index] = low.reshape(8, 4, 128)
            zs[8:16, index] = high.reshape(8, 4, 128)
        start(self.last_copies())

    def finish(self, outs, scale):
        z = self.pos[2]
        wait(self.last_copies())
        zb = self.ref("zb")
        total = (self.ref("zs")[z] + sum(zb[d - 1] for d in range(1, ZS))) * scale
        for index, out in enumerate(outs):
            out[...] = total[index]


def reduce_scratch(tag):
    dma = pltpu.SemaphoreType.DMA
    return {
        "x" + tag: pltpu.VMEM((2, YS, TILES, 8, 128), F32),
        "out" + tag: pltpu.VMEM((2, YS, TILES, 8, 128), F32),
        "bufc" + tag: pltpu.VMEM((YS, TILES, 8, 128), F32),
        "accc" + tag: pltpu.VMEM((YS, TILES, 8, 128), F32),
        "bufy" + tag: pltpu.VMEM((YS - 1, TILES, 8, 128), F32),
        "accy" + tag: pltpu.VMEM((TILES, 8, 128), F32),
        "bufz" + tag: pltpu.VMEM((ZS - 1, 8, 128), F32),
        "sc" + tag: dma((2,)),
        "rc" + tag: dma((2,)),
        "sy" + tag: dma((2, YS - 1)),
        "ry" + tag: dma((2, YS - 1)),
        "sz" + tag: dma((2, ZS - 1)),
        "rz" + tag: dma((2, ZS - 1)),
    }


def scatter_scratch(tag, n):
    dma = pltpu.SemaphoreType.DMA
    names = {}
    for kind in ("send", "got", "own"):
        names[kind + "x" + tag] = pltpu.VMEM((n, XS, YS, 32, 128), F32)
        names[kind + "y" + tag] = pltpu.VMEM((n, YS, XS, 32, 128), F32)
    for axis in ("x", "y"):
        names["b" + axis + tag] = pltpu.VMEM((n, 3, 4, 32, 128), F32)
        names["c" + axis + tag] = pltpu.VMEM((n, 4, 32, 128), F32)
        names["d" + axis + tag] = pltpu.VMEM((n, 3, 32, 128), F32)
    names["zs" + tag] = pltpu.VMEM((ZS, n, 4, 128), F32)
    names["zb" + tag] = pltpu.VMEM((ZS - 1, n, 4, 128), F32)
    for k in ("1", "2", "3"):
        shape = (2, n) if k == "1" else (2, n, 3)
        names["s" + k + tag] = dma(shape)
        names["r" + k + tag] = dma(shape)
    names["s4" + tag] = dma((ZS - 1,))
    names["r4" + tag] = dma((ZS - 1,))
    return names


def scratch():
    full = pltpu.VMEM((ROWS, D), F32)
    half = pltpu.VMEM((ROWS, D), BF16)
    names = {n: full for n in ("uq", "uk", "val", "fq", "fk", "att", "rden", "gnum", "gden", "wtd", "gin")}
    names.update({n: half for n in ("fqh", "fql", "fkh", "fkl", "vh", "vl", "gnh", "gnl", "gq", "gk", "gv")})
    names["gh"] = pltpu.VMEM((ROWS, F), F32)
    names["turn"] = pltpu.VMEM((2, QUAD, ROWS), BF16)
    names["ones"] = pltpu.VMEM((QUAD, QUAD), BF16)
    names["ph"] = pltpu.VMEM((2, QUAD, QUAD), BF16)
    names["pl"] = pltpu.VMEM((2, QUAD, QUAD), BF16)
    for n in ("sh", "sl", "gsh", "gsl"):
        names[n] = pltpu.VMEM((T, 2, QUAD, QUAD), BF16)
    names.update(reduce_scratch("_1"))
    names.update(reduce_scratch("_2"))
    names.update(scatter_scratch("_q", 1))
    names.update(scatter_scratch("_kv", 2))
    return names


def kernel(
    scale, x_ref, cot_ref, wq_ref, wk_ref, wv_ref, up_ref, down_ref, proj_ref, live_ref,
    gin_ref, oq_ref, ok_ref, ov_ref, *rest,
):
    r = dict(zip(scratch().keys(), rest))
    s = lax.axis_index("sensor")
    x, y, z, c = lax.axis_index("step"), s // (2 * ZS), lax.rem(s // 2, ZS), lax.rem(s, 2)
    pos = (x, y, z, c)
    peers = {
        "c": at(x, y, z, 1 - c),
        "y": [at(x, lax.rem(y + d, YS), z, c) for d in range(1, YS)],
        "x": [at(lax.rem(x + d, XS), y, z, c) for d in range(1, XS)],
        "z": [at(x, y, lax.rem(z + d, ZS), c) for d in range(1, ZS)],
    }
    everyone = [peers["c"]] + peers["y"] + peers["x"] + peers["z"]
    barrier = pltpu.get_barrier_semaphore()
    for target in everyone:
        pl.semaphore_signal(barrier, inc=1, device_id=target, device_id_type=MESH)

    rows = x_ref[...].reshape(ROWS, D)
    row_id = lax.rem(lax.broadcasted_iota(jnp.int32, (ROWS, 1), 0), N)
    valid = row_id < live_ref[0]
    quads = [pl.ds(QUAD * q, QUAD) for q in range(2)]
    moments = [pl.ds(N * t, N) for t in range(T)]

    same = lax.broadcasted_iota(jnp.int32, (QUAD, QUAD), 0) // E == lax.broadcasted_iota(jnp.int32, (QUAD, QUAD), 1) // E
    r["ones"][...] = jnp.where(same, 1.0, 0.0).astype(BF16)
    ones = r["ones"]
    zero = jnp.zeros((E, E), F32)
    for q in range(2):
        lines = []
        for k in range(4):
            parts = [zero] * 4
            parts[k] = proj_ref[4 * q + k]
            lines.append(jnp.concatenate(parts, axis=1))
        r["ph"][q], r["pl"][q] = split(jnp.concatenate(lines, axis=0))

    def features(u_ref, q):
        u = u_ref[:, quads[q]]
        exponent = dot3(dot, split(u), (r["ph"][q], r["pl"][q])) - 0.5 * head_sum(u * u, ones[...])
        return jnp.exp(exponent) * (E ** -0.5)

    def feature_back(weighted, u, q):
        back = dot3(dot_nt, split(weighted), (r["ph"][q], r["pl"][q])) - u * head_sum(weighted, ones[...])
        return (back * FACTOR).astype(BF16)

    r["uk"][...] = dot(rows, wk_ref[...]) * FACTOR
    r["val"][...] = dot(rows, wv_ref[...])
    r["vh"][...], r["vl"][...] = split(r["val"][...])
    for q in range(2):
        fk = jnp.where(valid, features(r["uk"], q), 0.0)
        r["fk"][:, quads[q]] = fk
        r["fkh"][:, quads[q]], r["fkl"][:, quads[q]] = split(fk)

    def outer(a, b, t, q):
        (ah, al), (bh, bl) = a, b
        here = moments[t], quads[q]
        left = jnp.concatenate([ah[here], al[here], ah[here]], axis=0)
        right = jnp.concatenate([bh[here], bh[here], bl[here]], axis=0)
        return dot_tn(left, right)

    first, second = Reduce(pos, peers, r, "_1"), Reduce(pos, peers, r, "_2")
    for ref in (first.x, second.x):
        ref[:, :, TILES - 1] = jnp.zeros((2, YS, 8, 128), F32)
    for t in range(T):
        for q in range(2):
            put_blocks(first.x, t, q, outer((r["fkh"], r["fkl"]), (r["vh"], r["vl"]), t, q))
        total = jnp.sum(r["fk"][moments[t], :], axis=0, keepdims=True)
        for p in range(PAIRS):
            put_row(first.x, t, p, total[:, 128 * p : 128 * p + 128])

    pl.semaphore_wait(barrier, len(everyone))
    first.start_core()
    r["uq"][...] = dot(rows, wq_ref[...]) * FACTOR
    first.start_y()
    for q in range(2):
        fq = features(r["uq"], q)
        r["fq"][:, quads[q]] = fq
        r["fqh"][:, quads[q]], r["fql"][:, quads[q]] = split(fq)
    first.start_z()
    masked = jnp.where(valid, cot_ref[...].reshape(ROWS, D), jnp.zeros((), BF16))
    r["gh"][...] = dot_nt(masked, down_ref[...])
    for n in ("sh", "sl", "gsh", "gsl"):
        r[n][...] = jnp.zeros_like(r[n])
    first.start_z_back()
    line = lax.broadcasted_iota(jnp.int32, (QUAD, D), 0)
    column = lax.broadcasted_iota(jnp.int32, (QUAD, D), 1)
    for k in range(2):
        source = (line // 64) * 128 + lax.rem(line // 4, ZS) * 8 + 4 * k + lax.rem(line, 4)
        pick = jnp.where(source == column, 1.0, 0.0).astype(BF16)
        r["turn"][k] = dot_nt(pick, rows).astype(BF16)
    first.start_y_back()
    first.start_core_back()
    first.finish()

    for t in range(T):
        for q in range(2):
            here = moments[t], quads[q]
            get_blocks(first.out, t, q, r["sh"], r["sl"])
            numer = dot3(dot, (r["fqh"][here], r["fql"][here]), (r["sh"][t, q], r["sl"][t, q]))
            inverse = 1.0 / head_sum(r["fq"][here] * get_row(first.out, t, q), ones[...])
            r["rden"][here] = inverse
            r["att"][here] = numer * inverse
    att = r["att"][...]
    rms_inverse = 1.0 / jnp.sqrt(jnp.mean(att * att, axis=1, keepdims=True) + 1e-06)
    normed = att * rms_inverse
    pre = dot(normed.astype(BF16), up_ref[...])
    grad_pre = (r["gh"][...] * gelu_slope(pre)).astype(BF16)
    grad_normed = dot_nt(grad_pre, up_ref[...])
    mean = jnp.mean(grad_normed * normed, axis=1, keepdims=True)
    grad_att = (grad_normed - normed * mean) * rms_inverse
    for q in range(2):
        ga = grad_att[:, QUAD * q : QUAD * q + QUAD]
        inverse = r["rden"][:, quads[q]]
        gnum = ga * inverse
        r["gnum"][:, quads[q]] = gnum
        r["gnh"][:, quads[q]], r["gnl"][:, quads[q]] = split(gnum)
        r["gden"][:, quads[q]] = -head_sum(ga * r["att"][:, quads[q]], ones[...]) * inverse
    for t in range(T):
        for q in range(2):
            put_blocks(second.x, t, q, outer((r["fqh"], r["fql"]), (r["gnh"], r["gnl"]), t, q))
        total = jnp.sum(r["fq"][moments[t], :] * r["gden"][moments[t], :], axis=0, keepdims=True)
        for p in range(PAIRS):
            put_row(second.x, t, p, total[:, 128 * p : 128 * p + 128])

    second.start_core()
    for t in range(T):
        for q in range(2):
            here = moments[t], quads[q]
            gfq = dot3(dot_nt, (r["gnh"][here], r["gnl"][here]), (r["sh"][t, q], r["sl"][t, q]))
            gfq = gfq + r["gden"][here] * get_row(first.out, t, q)
            r["wtd"][here] = gfq * r["fq"][here]
    second.start_y()
    for q in range(2):
        r["gq"][:, quads[q]] = feature_back(r["wtd"][:, quads[q]], r["uq"][:, quads[q]], q)
    job_q, job_kv = Scatter(pos, peers, r, "_q", 1), Scatter(pos, peers, r, "_kv", 2)
    job_q.put("send", 0, dot(r["turn"][1 - c], r["gq"][...]))
    second.start_z()
    start(job_q.core_copies(0))
    job_q.put("own", 0, dot(r["turn"][c], r["gq"][...]))
    job_q.start_second(0)
    r["gin"][...] = dot_nt(r["gq"][...], wq_ref[...])
    second.start_z_back()
    job_q.start_third(0)
    second.start_y_back()
    second.start_core_back()
    job_q.start_last()
    second.finish()

    for t in range(T):
        for q in range(2):
            here = moments[t], quads[q]
            get_blocks(second.out, t, q, r["gsh"], r["gsl"])
            blocks = (r["gsh"][t, q], r["gsl"][t, q])
            r["gv"][here] = dot3(dot, (r["fkh"][here], r["fkl"][here]), blocks).astype(BF16)
    job_kv.put("send", 1, dot(r["turn"][1 - c], r["gv"][...]))
    start(job_kv.core_copies(1))
    for t in range(T):
        for q in range(2):
            here = moments[t], quads[q]
            blocks = (r["gsh"][t, q], r["gsl"][t, q])
            gfk = dot3(dot_nt, (r["vh"][here], r["vl"][here]), blocks) + get_row(second.out, t, q)
            r["wtd"][here] = gfk * r["fk"][here]
    for q in range(2):
        r["gk"][:, quads[q]] = feature_back(r["wtd"][:, quads[q]], r["uk"][:, quads[q]], q)
    job_kv.put("send", 0, dot(r["turn"][1 - c], r["gk"][...]))
    start(job_kv.core_copies(0))
    job_kv.put("own", 1, dot(r["turn"][c], r["gv"][...]))
    job_kv.start_second(1)
    job_kv.put("own", 0, dot(r["turn"][c], r["gk"][...]))
    job_kv.start_second(0)
    total = r["gin"][...] + dot_nt(r["gk"][...], wk_ref[...]) + dot_nt(r["gv"][...], wv_ref[...])
    gin_ref[...] = total.astype(BF16).reshape(T, N, D)
    job_q.finish((oq_ref,), scale)
    job_kv.start_third(1)
    job_kv.start_third(0)
    job_kv.start_last()
    job_kv.finish((ok_ref, ov_ref), scale)
    first.drain()
    second.drain()


def shards(inputs, cotangent, w_query, w_key, w_value, w_up, w_down, feature_proj, live_count):
    total_rows = T * XS * N * YS * ZS * 2
    piece = jax.ShapeDtypeStruct((4, 128), F32)
    return pl.pallas_call(
        functools.partial(kernel, 1.0 / math.sqrt(total_rows)),
        out_shape=(jax.ShapeDtypeStruct((T, N, D), BF16), piece, piece, piece),
        in_specs=[VM] * 8 + [SM],
        out_specs=(VM,) * 4,
        scratch_shapes=list(scratch().values()),
        compiler_params=pltpu.CompilerParams(collective_id=0, has_side_effects=True, vmem_limit_bytes=56 << 20),
    )(inputs, cotangent, w_query, w_key, w_value, w_up, w_down, feature_proj, live_count)


def solution(mesh):
    placed = (P("step", "sensor", None),) * 2 + (P(),) * 6 + (P("sensor"),)
    return jax.shard_map(
        shards,
        mesh=mesh,
        in_specs=placed,
        out_specs=(P("step", "sensor", None),) + (P("sensor", "step"),) * 3,
        check_vma=False,
    )
```

time: 1840 us -> 105 us (0.06)
  blocking collectives: 989 us -> 0 us
  waiting for transfers between devices: 754 us -> 0 us
  Pallas kernels: 0 us -> 99.2 us
  matrix products: 33.7 us -> 0 us
  local copies, waits for them, and re-layouts: 35.4 us -> 3.55 us
    psum x2 -> x0, blocking collectives: 989 us -> none  [the longest x1 498 us: shards(): lax.psum((local_summary[moment], local_normal[moment]), 'sensor')]
    unnamed x7 -> x0, waiting for transfers between devices: 346 us -> none
    psum x2 -> x0, waiting for transfers between devices: 326 us -> none  [the longest x1 326 us: shards(): lax.psum((local_gsum[moment], local_gnorm[moment]), 'sensor')]
    pallas_call x0 -> x1, Pallas kernels: none -> 99.2 us  [shards(): pl.pallas_call(functools.partial(kernel, 1.0 / math.sqrt(total_rows)), ou...]
    reduce_scatter x3 -> x0, waiting for transfers between devices: 82.3 us -> none  [the longest x1 30.1 us: shards(): lax.psum_scatter(partial_sums[1], 'step', scatter_dimension=1, tiled=True)]
    dot_general x23 -> x0, matrix products: 33.7 us -> none  [the longest x2 4.52 us: feature_back(): jnp.einsum('...hr,her->...he', weighted, feature_proj, precision=HIGH)]
  transfers between devices with their start and end apart: 6 -> 0, of which waited for: 5 -> 0; matrix products, arithmetic and copies ran while one was open for 1% -> 0% of each run, Pallas kernels for 0% -> 0%
where the time goes in v2:
time: 105 us; the launch traced here: 104 us
  Pallas kernels  99.2 us (94%)
  local copies, waits for them, and re-layouts  3.55 us (3%)
  between operations  1.3 us (1%)
    pallas_call x1, Pallas kernels, shards(): pl.pallas_call(functools.partial(kernel, 1.0 / math.sqrt(total_rows)), ou...  99.2 us
    unnamed x10, local copies, waits for them, and re-layouts  3.55 us

profile of v2, /device:TPU:1, one launch (start us, length us, event | category | flops | bytes accessed | tf_op | source)
XLA Modules:
  0.0 104.1 jit_solution(17535300039623301505)
XLA Ops:
  1.3 99.2 %shard_map.120 = (bf16[3,64,512]{2,1,0:T(8,128)(2,1)}, f32[4,128]{1,0:T(4,128)}, f32[4,128]{1,0:T(4,128)}, f32[4,128]{1,0:T(4,128)}) custom-call(bf16[3,64,512]{2,1,0:T(8,128)(2,1)} %x_ref.1, bf16[3,64,512]{2,1,0:T(8,128)(2,1)} %cot_ref.1, bf16[512,512]{1,0:T(8,128)(2,1)} %wq_ref.1, bf16[512,512]{1,0:T(8,128)(2,1)} %wk_ref.1, bf16[512,512]{1,0:T(8,128)(2,1)} %wv_ref.1, ...), custom_call_target="tpu_custom_call" | custom-call | tf_op jit(solution)/shard_map/pallas_call | solution.py:573
  100.5 0.0 copy-start.2
  100.5 1.6 %copy.18 = bf16[3,64,512]{2,1,0:T(8,128)(2,1)} copy(bf16[3,64,512]{2,1,0:T(8,128)(2,1)} %get-tuple-element.8) | data formatting | bytes 393216
  102.2 0.0 copy-done.2
  102.2 0.0 copy-start.1
  102.2 0.6 copy.19
  102.7 0.1 copy-done.1
  102.8 0.0 copy-start
  102.8 0.6 copy.20
  103.4 0.1 copy-done
  103.5 0.6 copy.21
Async XLA Ops:
  100.5 1.6 %copy-start.2 = (f32[4,128]{1,0:T(4,128)S(1)}, f32[4,128]{1,0:T(4,128)}, u32[]{:S(2)}) copy-start(f32[4,128]{1,0:T(4,128)} %get-tuple-element.9) | copy-start | bytes 6148
  102.2 0.7 copy-start.1
  102.8 0.7 copy-start

commit v3 on v2

--- a/solution.py
+++ b/solution.py
@@ -10,7 +10,7 @@
 
 MESH = pl.DeviceIdType.MESH
 VM = pl.BlockSpec(memory_space=pltpu.VMEM)
-SM = pl.BlockSpec(memory_space=pltpu.SMEM)
+ANY = pl.BlockSpec(memory_space=pl.ANY)
 F32, BF16 = jnp.float32, jnp.bfloat16
 YS, ZS, XS = 4, 16, 4
 T, N, D, F, H, E = 3, 64, 512, 256, 8, 64
@@ -19,6 +19,19 @@
 TILES = 13
 QUAD = 256
 FACTOR = E ** (-0.25)
+STAGED = {
+    "x": ((T, N, D), BF16),
+    "wk": ((D, D), BF16),
+    "proj": ((H, E, E), F32),
+    "wv": ((D, D), BF16),
+    "live": ((1,), jnp.int32),
+    "wq": ((D, D), BF16),
+    "cot": ((T, N, D), BF16),
+    "down": ((F, D), BF16),
+    "up": ((D, F), BF16),
+}
+FAR_4 = (2, 1, 3)
+FAR_16 = (8, 7, 9, 6, 10, 5, 11, 4, 12, 3, 13, 2, 14, 1, 15)
 
 
 def at(x, y, z, c):
@@ -82,23 +95,18 @@
         self.sc, self.rc, self.sy, self.ry = r["sc" + tag], r["rc" + tag], r["sy" + tag], r["ry" + tag]
         self.sz, self.rz = r["sz" + tag], r["rz" + tag]
 
-    def start_core(self):
-        c = self.pos[3]
-        self.core = send(self.x.at[1 - c], self.buf_c, self.sc.at[0], self.rc.at[0], self.peers["c"])
-        self.core.start()
-
-    def start_y(self):
-        _, y, _, c = self.pos
-        self.core.wait()
-        self.acc_c[...] = self.x[c] + self.buf_c[...]
-        self.down = [
-            send(
-                self.acc_c.at[lax.rem(y + d, YS)], self.buf_y.at[d - 1], self.sy.at[0, d - 1], self.ry.at[0, d - 1],
-                self.peers["y"][d - 1],
-            )
-            for d in range(1, YS)
-        ]
-        start(self.down)
+    def core_down(self, k):
+        chunk = lax.rem(self.pos[1] + k, YS)
+        return send(
+            self.x.at[1 - self.pos[3], chunk], self.buf_c.at[chunk], self.sc.at[0, k], self.rc.at[0, k], self.peers["c"]
+        )
+
+    def y_down(self, d):
+        chunk = lax.rem(self.pos[1] + d, YS)
+        return send(
+            self.acc_c.at[chunk], self.buf_y.at[d - 1], self.sy.at[0, d - 1], self.ry.at[0, d - 1],
+            self.peers["y"][d - 1],
+        )
 
     def z_down(self, d, slot):
         return send(
@@ -109,11 +117,32 @@
         piece = self.out.at[self.pos[3], self.pos[1], slot]
         return send(piece, piece, self.sz.at[1, d - 1], self.rz.at[1, d - 1], self.peers["z"][d - 1])
 
+    def y_up(self, d, piece):
+        return send(piece, piece, self.sy.at[1, d - 1], self.ry.at[1, d - 1], self.peers["y"][d - 1])
+
+    def core_up(self, k, group):
+        piece = self.out.at[self.pos[3], group]
+        return send(piece, piece, self.sc.at[1, k], self.rc.at[1, k], self.peers["c"])
+
+    def start_core(self):
+        for k in FAR_4 + (0,):
+            self.core_down(k).start()
+
+    def start_y(self):
+        _, y, _, c = self.pos
+        for k in FAR_4 + (0,):
+            self.core_down(k).wait()
+            chunk = lax.rem(y + k, YS)
+            self.acc_c[chunk] = self.x[c, chunk] + self.buf_c[chunk]
+            if k:
+                self.y_down(k).start()
+
     def start_z(self):
         _, y, z, _ = self.pos
-        wait(self.down)
+        for d in range(1, YS):
+            self.y_down(d).wait()
         self.acc_y[...] = self.acc_c[y] + self.buf_y[0] + self.buf_y[1] + self.buf_y[2]
-        for d in range(1, ZS):
+        for d in FAR_16:
             other = lax.rem(z + d, ZS)
 
             @pl.when(other < TILES)
@@ -128,36 +157,38 @@
             for d in range(1, ZS):
                 self.z_down(d, 0).wait_recv()
             self.out[c, y, z] = self.acc_y[z] + sum(self.buf_z[d - 1] for d in range(1, ZS))
-            for d in range(1, ZS):
+            for d in FAR_16:
                 self.z_up(d, z).start()
+            for d in FAR_4:
+                self.y_up(d, self.out.at[c, y, z]).start()
 
     def start_y_back(self):
         _, y, z, c = self.pos
-        for d in range(1, ZS):
+        for d in FAR_16[::-1]:
             source = lax.rem(z + ZS - d, ZS)
 
             @pl.when(source < TILES)
             def _():
                 self.z_up(d, source).wait_recv()
-
-        mine = self.out.at[c, y]
-        self.up = [
-            send(mine, mine, self.sy.at[1, d - 1], self.ry.at[1, d - 1], self.peers["y"][d - 1]) for d in range(1, YS)
-        ]
-        start(self.up)
+                for e in FAR_4:
+                    self.y_up(e, self.out.at[c, y, source]).start()
 
     def start_core_back(self):
-        c = self.pos[3]
-        wait(self.up)
-        mine = self.out.at[c]
-        self.core = send(mine, mine, self.sc.at[1], self.rc.at[1], self.peers["c"])
-        self.core.start()
+        _, y, _, c = self.pos
+        self.core_up(0, y).start()
+        for d in (1, 3, 2):
+            group = lax.rem(y + YS - d, YS)
+            self.y_up(d, self.out.at[c, group]).wait_recv()
+            self.core_up(d, group).start()
 
     def finish(self):
-        self.core.wait()
+        for k in range(YS):
+            group = lax.rem(self.pos[1] + YS - k, YS)
+            piece = self.out.at[1 - self.pos[3], group]
+            send(piece, piece, self.sc.at[1, k], self.rc.at[1, k], self.peers["c"]).wait_recv()
 
     def drain(self):
-        z = self.pos[2]
+        _, y, z, c = self.pos
         for d in range(1, ZS):
             other = lax.rem(z + d, ZS)
 
@@ -169,6 +200,11 @@
         def _():
             for d in range(1, ZS):
                 self.z_up(d, z).wait_send()
+
+        for d in range(1, YS):
+            self.y_up(d, self.out.at[c, y]).wait_send()
+        for k in range(YS):
+            self.core_up(k, lax.rem(y + YS - k, YS)).wait_send()
 
 
 def tile_place(tile):
@@ -221,109 +257,93 @@
 
 
 class Scatter:
-    def __init__(self, pos, peers, r, tag, count):
-        self.pos, self.peers, self.count, self.r, self.tag = pos, peers, count, r, tag
+    def __init__(self, pos, peers, r, tag):
+        self.pos, self.peers, self.r, self.tag = pos, peers, r, tag
 
     def ref(self, name):
         return self.r[name + self.tag]
 
-    def put(self, name, index, result):
+    def put(self, name, result):
         xf, yf = self.ref(name + "x"), self.ref(name + "y")
         for y in range(YS):
             for x in range(XS):
                 block = result[64 * y : 64 * y + 64, 128 * x : 128 * x + 128]
-                xf[index, x, y] = block[0:32]
-                yf[index, y, x] = block[32:64]
-
-    def core_copies(self, index):
-        s, q = self.ref("s1"), self.ref("r1")
-        return [
-            send(self.ref("sendx").at[index], self.ref("gotx").at[index], s.at[0, index], q.at[0, index], self.peers["c"]),
-            send(self.ref("sendy").at[index], self.ref("goty").at[index], s.at[1, index], q.at[1, index], self.peers["c"]),
-        ]
-
-    def second_copies(self, index):
-        x, y, _, _ = self.pos
-        s, q = self.ref("s2"), self.ref("r2")
-        copies = []
-        for d in range(1, XS):
-            copies.append(
-                send(
-                    self.ref("ownx").at[index, lax.rem(x + d, XS)], self.ref("bx").at[index, d - 1],
-                    s.at[0, index, d - 1], q.at[0, index, d - 1], self.peers["x"][d - 1],
-                )
-            )
-            copies.append(
-                send(
-                    self.ref("owny").at[index, lax.rem(y + d, YS)], self.ref("by").at[index, d - 1],
-                    s.at[1, index, d - 1], q.at[1, index, d - 1], self.peers["y"][d - 1],
-                )
-            )
-        return copies
-
-    def start_second(self, index):
-        wait(self.core_copies(index))
-        for name in ("x", "y"):
-            own, got = self.ref("own" + name), self.ref("got" + name)
-            own[index] = own[index] + got[index]
-        start(self.second_copies(index))
-
-    def third_copies(self, index):
-        x, y, _, _ = self.pos
-        s, q = self.ref("s3"), self.ref("r3")
-        copies = []
-        for d in range(1, XS):
-            copies.append(
-                send(
-                    self.ref("cx").at[index, lax.rem(y + d, YS)], self.ref("dx").at[index, d - 1],
-                    s.at[0, index, d - 1], q.at[0, index, d - 1], self.peers["y"][d - 1],
-                )
-            )
-            copies.append(
-                send(
-                    self.ref("cy").at[index, lax.rem(x + d, XS)], self.ref("dy").at[index, d - 1],
-                    s.at[1, index, d - 1], q.at[1, index, d - 1], self.peers["x"][d - 1],
-                )
-            )
-        return copies
-
-    def start_third(self, index):
-        x, y, _, _ = self.pos
-        wait(self.second_copies(index))
-        bx, by = self.ref("bx"), self.ref("by")
-        self.ref("cx")[index] = self.ref("ownx")[index, x] + bx[index, 0] + bx[index, 1] + bx[index, 2]
-        self.ref("cy")[index] = self.ref("owny")[index, y] + by[index, 0] + by[index, 1] + by[index, 2]
-        start(self.third_copies(index))
-
-    def last_copies(self):
-        z = self.pos[2]
-        return [
-            send(
-                self.ref("zs").at[lax.rem(z + d, ZS)], self.ref("zb").at[d - 1],
-                self.ref("s4").at[d - 1], self.ref("r4").at[d - 1], self.peers["z"][d - 1],
-            )
-            for d in range(1, ZS)
-        ]
+                xf[x, y] = block[0:32]
+                yf[y, x] = block[32:64]
+
+    def sems(self, phase, half, k):
+        return self.ref("s" + phase).at[half, k], self.ref("r" + phase).at[half, k]
+
+    def chunk(self, half, k):
+        return lax.rem(self.pos[half] + k, 4)
+
+    def core_copy(self, half, k):
+        name, chunk = "xy"[half], self.chunk(half, k)
+        return send(
+            self.ref("send" + name).at[chunk], self.ref("got" + name).at[chunk], *self.sems("1", half, k), self.peers["c"]
+        )
+
+    def second_copy(self, half, d):
+        name = "xy"[half]
+        return send(
+            self.ref("own" + name).at[self.chunk(half, d)], self.ref("b" + name).at[d - 1],
+            *self.sems("2", half, d - 1), self.peers[name][d - 1],
+        )
+
+    def third_copy(self, half, d):
+        name, other = "xy"[half], "yx"[half]
+        return send(
+            self.ref("c" + name).at[self.chunk(1 - half, d)], self.ref("d" + name).at[d - 1],
+            *self.sems("3", half, d - 1), self.peers[other][d - 1],
+        )
+
+    def last_copy(self, d):
+        return send(
+            self.ref("zs").at[lax.rem(self.pos[2] + d, ZS)], self.ref("zb").at[d - 1],
+            self.ref("s4").at[d - 1], self.ref("r4").at[d - 1], self.peers["z"][d - 1],
+        )
+
+    def start_core(self):
+        for k in FAR_4 + (0,):
+            for half in range(2):
+                self.core_copy(half, k).start()
+
+    def start_second(self):
+        for k in FAR_4 + (0,):
+            for half in range(2):
+                self.core_copy(half, k).wait()
+                own, got = self.ref("own" + "xy"[half]), self.ref("got" + "xy"[half])
+                chunk = self.chunk(half, k)
+                own[chunk] = own[chunk] + got[chunk]
+                if k:
+                    self.second_copy(half, k).start()
+
+    def start_third(self):
+        for half in range(2):
+            name = "xy"[half]
+            for d in range(1, 4):
+                self.second_copy(half, d).wait()
+            got = self.ref("b" + name)
+            self.ref("c" + name)[...] = self.ref("own" + name)[self.pos[half]] + got[0] + got[1] + got[2]
+            for d in FAR_4:
+                self.third_copy(half, d).start()
 
     def start_last(self):
-        x, y, _, _ = self.pos
         zs = self.ref("zs")
-        for index in range(self.count):
-            wait(self.third_copies(index))
-            dx, dy = self.ref("dx"), self.ref("dy")
-            low = self.ref("cx")[index, y] + dx[index, 0] + dx[index, 1] + dx[index, 2]
-            high = self.ref("cy")[index, x] + dy[index, 0] + dy[index, 1] + dy[index, 2]
-            zs[0:8, index] = low.reshape(8, 4, 128)
-            zs[8:16, index] = high.reshape(8, 4, 128)
-        start(self.last_copies())
-
-    def finish(self, outs, scale):
-        z = self.pos[2]
-        wait(self.last_copies())
+        for half in range(2):
+            for d in range(1, 4):
+                self.third_copy(half, d).wait()
+            got = self.ref("d" + "xy"[half])
+            total = self.ref("c" + "xy"[half])[self.pos[1 - half]] + got[0] + got[1] + got[2]
+            zs[8 * half : 8 * half + 8] = total.reshape(8, 4, 128)
+        for d in FAR_16:
+            self.last_copy(d).start()
+
+    def finish(self, out, scale):
+        for d in range(1, ZS):
+            self.last_copy(d).wait()
         zb = self.ref("zb")
-        total = (self.ref("zs")[z] + sum(zb[d - 1] for d in range(1, ZS))) * scale
-        for index, out in enumerate(outs):
-            out[...] = total[index]
+        out[...] = (self.ref("zs")[self.pos[2]] + sum(zb[d - 1] for d in range(1, ZS))) * scale
 
 
 def reduce_scratch(tag):
@@ -336,8 +356,8 @@
         "bufy" + tag: pltpu.VMEM((YS - 1, TILES, 8, 128), F32),
         "accy" + tag: pltpu.VMEM((TILES, 8, 128), F32),
         "bufz" + tag: pltpu.VMEM((ZS - 1, 8, 128), F32),
-        "sc" + tag: dma((2,)),
-        "rc" + tag: dma((2,)),
+        "sc" + tag: dma((2, YS)),
+        "rc" + tag: dma((2, YS)),
         "sy" + tag: dma((2, YS - 1)),
         "ry" + tag: dma((2, YS - 1)),
         "sz" + tag: dma((2, ZS - 1)),
@@ -345,22 +365,20 @@
     }
 
 
-def scatter_scratch(tag, n):
+def scatter_scratch(tag):
     dma = pltpu.SemaphoreType.DMA
     names = {}
-    for kind in ("send", "got", "own"):
-        names[kind + "x" + tag] = pltpu.VMEM((n, XS, YS, 32, 128), F32)
-        names[kind + "y" + tag] = pltpu.VMEM((n, YS, XS, 32, 128), F32)
     for axis in ("x", "y"):
-        names["b" + axis + tag] = pltpu.VMEM((n, 3, 4, 32, 128), F32)
-        names["c" + axis + tag] = pltpu.VMEM((n, 4, 32, 128), F32)
-        names["d" + axis + tag] = pltpu.VMEM((n, 3, 32, 128), F32)
-    names["zs" + tag] = pltpu.VMEM((ZS, n, 4, 128), F32)
-    names["zb" + tag] = pltpu.VMEM((ZS - 1, n, 4, 128), F32)
+        for kind in ("send", "got", "own"):
+            names[kind + axis + tag] = pltpu.VMEM((4, 4, 32, 128), F32)
+        names["b" + axis + tag] = pltpu.VMEM((3, 4, 32, 128), F32)
+        names["c" + axis + tag] = pltpu.VMEM((4, 32, 128), F32)
+        names["d" + axis + tag] = pltpu.VMEM((3, 32, 128), F32)
+    names["zs" + tag] = pltpu.VMEM((ZS, 4, 128), F32)
+    names["zb" + tag] = pltpu.VMEM((ZS - 1, 4, 128), F32)
     for k in ("1", "2", "3"):
-        shape = (2, n) if k == "1" else (2, n, 3)
-        names["s" + k + tag] = dma(shape)
-        names["r" + k + tag] = dma(shape)
+        names["s" + k + tag] = dma((2, 4))
+        names["r" + k + tag] = dma((2, 4))
     names["s4" + tag] = dma((ZS - 1,))
     names["r4" + tag] = dma((ZS - 1,))
     return names
@@ -369,7 +387,7 @@
 def scratch():
     full = pltpu.VMEM((ROWS, D), F32)
     half = pltpu.VMEM((ROWS, D), BF16)
-    names = {n: full for n in ("uq", "uk", "val", "fq", "fk", "att", "rden", "gnum", "gden", "wtd", "gin")}
+    names = {n: full for n in ("uq", "uk", "fq", "fk", "att", "rden", "gnum", "gden", "wtd", "gin")}
     names.update({n: half for n in ("fqh", "fql", "fkh", "fkl", "vh", "vl", "gnh", "gnl", "gq", "gk", "gv")})
     names["gh"] = pltpu.VMEM((ROWS, F), F32)
     names["turn"] = pltpu.VMEM((2, QUAD, ROWS), BF16)
@@ -380,16 +398,31 @@
         names[n] = pltpu.VMEM((T, 2, QUAD, QUAD), BF16)
     names.update(reduce_scratch("_1"))
     names.update(reduce_scratch("_2"))
-    names.update(scatter_scratch("_q", 1))
-    names.update(scatter_scratch("_kv", 2))
+    for tag in ("_q", "_k", "_v"):
+        names.update(scatter_scratch(tag))
+    for n, (shape, kind) in STAGED.items():
+        names["in_" + n] = pltpu.SMEM(shape, kind) if n == "live" else pltpu.VMEM(shape, kind)
+    names["fetch"] = pltpu.SemaphoreType.DMA((len(STAGED),))
     return names
 
 
 def kernel(
-    scale, x_ref, cot_ref, wq_ref, wk_ref, wv_ref, up_ref, down_ref, proj_ref, live_ref,
+    scale, x_hbm, cot_hbm, wq_hbm, wk_hbm, wv_hbm, up_hbm, down_hbm, proj_hbm, live_hbm,
     gin_ref, oq_ref, ok_ref, ov_ref, *rest,
 ):
     r = dict(zip(scratch().keys(), rest))
+    sources = dict(
+        x=x_hbm, cot=cot_hbm, wq=wq_hbm, wk=wk_hbm, wv=wv_hbm, up=up_hbm, down=down_hbm, proj=proj_hbm, live=live_hbm
+    )
+    fetches = {
+        n: pltpu.make_async_copy(sources[n], r["in_" + n], r["fetch"].at[i]) for i, n in enumerate(STAGED)
+    }
+    start(fetches.values())
+
+    def fetched(n):
+        fetches[n].wait()
+        return r["in_" + n]
+
     s = lax.axis_index("sensor")
     x, y, z, c = lax.axis_index("step"), s // (2 * ZS), lax.rem(s // 2, ZS), lax.rem(s, 2)
     pos = (x, y, z, c)
@@ -404,9 +437,7 @@
     for target in everyone:
         pl.semaphore_signal(barrier, inc=1, device_id=target, device_id_type=MESH)
 
-    rows = x_ref[...].reshape(ROWS, D)
     row_id = lax.rem(lax.broadcasted_iota(jnp.int32, (ROWS, 1), 0), N)
-    valid = row_id < live_ref[0]
     quads = [pl.ds(QUAD * q, QUAD) for q in range(2)]
     moments = [pl.ds(N * t, N) for t in range(T)]
 
@@ -414,6 +445,9 @@
     r["ones"][...] = jnp.where(same, 1.0, 0.0).astype(BF16)
     ones = r["ones"]
     zero = jnp.zeros((E, E), F32)
+    rows = fetched("x")[...].reshape(ROWS, D)
+    r["uk"][...] = dot(rows, fetched("wk")[...]) * FACTOR
+    proj_ref = fetched("proj")
     for q in range(2):
         lines = []
         for k in range(4):
@@ -431,9 +465,8 @@
         back = dot3(dot_nt, split(weighted), (r["ph"][q], r["pl"][q])) - u * head_sum(weighted, ones[...])
         return (back * FACTOR).astype(BF16)
 
-    r["uk"][...] = dot(rows, wk_ref[...]) * FACTOR
-    r["val"][...] = dot(rows, wv_ref[...])
-    r["vh"][...], r["vl"][...] = split(r["val"][...])
+    r["vh"][...], r["vl"][...] = split(dot(rows, fetched("wv")[...]))
+    valid = row_id < fetched("live")[0]
     for q in range(2):
         fk = jnp.where(valid, features(r["uk"], q), 0.0)
         r["fk"][:, quads[q]] = fk
@@ -458,6 +491,7 @@
 
     pl.semaphore_wait(barrier, len(everyone))
     first.start_core()
+    wq_ref = fetched("wq")
     r["uq"][...] = dot(rows, wq_ref[...]) * FACTOR
     first.start_y()
     for q in range(2):
@@ -465,8 +499,9 @@
         r["fq"][:, quads[q]] = fq
         r["fqh"][:, quads[q]], r["fql"][:, quads[q]] = split(fq)
     first.start_z()
-    masked = jnp.where(valid, cot_ref[...].reshape(ROWS, D), jnp.zeros((), BF16))
-    r["gh"][...] = dot_nt(masked, down_ref[...])
+    masked = jnp.where(valid, fetched("cot")[...].reshape(ROWS, D), jnp.zeros((), BF16))
+    r["gh"][...] = dot_nt(masked, fetched("down")[...])
+    up_ref = fetched("up")
     for n in ("sh", "sl", "gsh", "gsl"):
         r[n][...] = jnp.zeros_like(r[n])
     first.start_z_back()
@@ -520,15 +555,15 @@
     second.start_y()
     for q in range(2):
         r["gq"][:, quads[q]] = feature_back(r["wtd"][:, quads[q]], r["uq"][:, quads[q]], q)
-    job_q, job_kv = Scatter(pos, peers, r, "_q", 1), Scatter(pos, peers, r, "_kv", 2)
-    job_q.put("send", 0, dot(r["turn"][1 - c], r["gq"][...]))
+    job_q, job_k, job_v = (Scatter(pos, peers, r, tag) for tag in ("_q", "_k", "_v"))
+    job_q.put("send", dot(r["turn"][1 - c], r["gq"][...]))
     second.start_z()
-    start(job_q.core_copies(0))
-    job_q.put("own", 0, dot(r["turn"][c], r["gq"][...]))
-    job_q.start_second(0)
+    job_q.start_core()
+    job_q.put("own", dot(r["turn"][c], r["gq"][...]))
+    job_q.start_second()
     r["gin"][...] = dot_nt(r["gq"][...], wq_ref[...])
     second.start_z_back()
-    job_q.start_third(0)
+    job_q.start_third()
     second.start_y_back()
     second.start_core_back()
     job_q.start_last()
@@ -540,8 +575,8 @@
             get_blocks(second.out, t, q, r["gsh"], r["gsl"])
             blocks = (r["gsh"][t, q], r["gsl"][t, q])
             r["gv"][here] = dot3(dot, (r["fkh"][here], r["fkl"][here]), blocks).astype(BF16)
-    job_kv.put("send", 1, dot(r["turn"][1 - c], r["gv"][...]))
-    start(job_kv.core_copies(1))
+    job_v.put("send", dot(r["turn"][1 - c], r["gv"][...]))
+    job_v.start_core()
     for t in range(T):
         for q in range(2):
             here = moments[t], quads[q]
@@ -550,34 +585,51 @@
             r["wtd"][here] = gfk * r["fk"][here]
     for q in range(2):
         r["gk"][:, quads[q]] = feature_back(r["wtd"][:, quads[q]], r["uk"][:, quads[q]], q)
-    job_kv.put("send", 0, dot(r["turn"][1 - c], r["gk"][...]))
-    start(job_kv.core_copies(0))
-    job_kv.put("own", 1, dot(r["turn"][c], r["gv"][...]))
-    job_kv.start_second(1)
-    job_kv.put("own", 0, dot(r["turn"][c], r["gk"][...]))
-    job_kv.start_second(0)
-    total = r["gin"][...] + dot_nt(r["gk"][...], wk_ref[...]) + dot_nt(r["gv"][...], wv_ref[...])
+    job_k.put("send", dot(r["turn"][1 - c], r["gk"][...]))
+    job_k.start_core()
+    job_v.put("own", dot(r["turn"][c], r["gv"][...]))
+    job_v.start_second()
+    job_k.put("own", dot(r["turn"][c], r["gk"][...]))
+    job_k.start_second()
+    total = r["gin"][...] + dot_nt(r["gk"][...], r["in_wk"][...]) + dot_nt(r["gv"][...], r["in_wv"][...])
     gin_ref[...] = total.astype(BF16).reshape(T, N, D)
-    job_q.finish((oq_ref,), scale)
-    job_kv.start_third(1)
-    job_kv.start_third(0)
-    job_kv.start_last()
-    job_kv.finish((ok_ref, ov_ref), scale)
+    job_v.start_third()
+    job_k.start_third()
+    job_v.start_last()
+    job_k.start_last()
+    job_q.finish(oq_ref, scale)
+    job_v.finish(ov_ref, scale)
+    job_k.finish(ok_ref, scale)
     first.drain()
     second.drain()
+
+
+def hand_on(*refs):
+    ins, outs, sem = refs[:4], refs[4:8], refs[8]
+    copies = [pltpu.make_async_copy(a, b, sem.at[i]) for i, (a, b) in enumerate(zip(ins, outs))]
+    start(copies)
+    wait(copies)
 
 
 def shards(inputs, cotangent, w_query, w_key, w_value, w_up, w_down, feature_proj, live_count):
     total_rows = T * XS * N * YS * ZS * 2
     piece = jax.ShapeDtypeStruct((4, 128), F32)
-    return pl.pallas_call(
+    shapes = (jax.ShapeDtypeStruct((T, N, D), BF16), piece, piece, piece)
+    results = pl.pallas_call(
         functools.partial(kernel, 1.0 / math.sqrt(total_rows)),
-        out_shape=(jax.ShapeDtypeStruct((T, N, D), BF16), piece, piece, piece),
-        in_specs=[VM] * 8 + [SM],
+        out_shape=shapes,
+        in_specs=[ANY] * 8 + [pl.BlockSpec(memory_space=pltpu.HBM)],
         out_specs=(VM,) * 4,
         scratch_shapes=list(scratch().values()),
         compiler_params=pltpu.CompilerParams(collective_id=0, has_side_effects=True, vmem_limit_bytes=56 << 20),
     )(inputs, cotangent, w_query, w_key, w_value, w_up, w_down, feature_proj, live_count)
+    return pl.pallas_call(
+        hand_on,
+        out_shape=shapes,
+        in_specs=[ANY] * 4,
+        out_specs=(ANY,) * 4,
+        scratch_shapes=[pltpu.SemaphoreType.DMA((4,))],
+    )(*results)
 
 
 def solution(mesh):

time: 105 us -> 101 us (0.962)
  local copies, waits for them, and re-layouts: 3.55 us -> 0 us
    pallas_call x0 -> x1, Pallas kernels: none -> 7.28 us  [shards(): pl.pallas_call(hand_on, out_shape=shapes, in_specs=[ANY] * 4, out_specs=(...]
    pallas_call x1, Pallas kernels: 99.2 us -> 92.4 us  [shards(): pl.pallas_call(functools.partial(kernel, 1.0 / math.sqrt(total_rows)), ou...]
    unnamed x10 -> x0, local copies, waits for them, and re-layouts: 3.55 us -> none
where the time goes in v3:
time: 101 us
  Pallas kernels  99.7 us (99%)
  between operations  1.29 us (1%)
    pallas_call x1, Pallas kernels, shards(): pl.pallas_call(functools.partial(kernel, 1.0 / math.sqrt(total_rows)), ou...  92.4 us
    pallas_call x1, Pallas kernels, shards(): pl.pallas_call(hand_on, out_shape=shapes, in_specs=[ANY] * 4, out_specs=(...  7.28 us

profile of v3, /device:TPU:1, one launch (start us, length us, event | category | flops | bytes accessed | tf_op | source)
XLA Modules:
  0.0 101.0 jit_solution(16099703850843831468)
XLA Ops:
  1.3 92.4 %shard_map.120 = (bf16[3,64,512]{2,1,0:T(8,128)(2,1)}, f32[4,128]{1,0:T(4,128)}, f32[4,128]{1,0:T(4,128)}, f32[4,128]{1,0:T(4,128)}) custom-call(bf16[3,64,512]{2,1,0:T(8,128)(2,1)} %x_hbm.1, bf16[3,64,512]{2,1,0:T(8,128)(2,1)} %cot_hbm.1, bf16[512,512]{1,0:T(8,128)(2,1)} %wq_hbm.1, bf16[512,512]{1,0:T(8,128)(2,1)} %wk_hbm.1, bf16[512,512]{1,0:T(8,128)(2,1)} %wv_hbm.1, ...), custom_call_target="tpu_custom_call" | custom-call | tf_op jit(solution)/shard_map/pallas_call | solution.py:618
  93.7 7.3 %shard_map.121 = (bf16[3,64,512]{2,1,0:T(8,128)(2,1)}, f32[4,128]{1,0:T(4,128)}, f32[4,128]{1,0:T(4,128)}, f32[4,128]{1,0:T(4,128)}) custom-call(bf16[3,64,512]{2,1,0:T(8,128)(2,1)} %get-tuple-element.8.refs_0_, f32[4,128]{1,0:T(4,128)} %get-tuple-element.9.refs_1_, f32[4,128]{1,0:T(4,128)} %get-tuple-element.10.refs_2_, f32[4,128]{1,0:T(4,128)} %get-tuple-element.11.refs_3_), custom_call_target="tpu_custom_call" | custom-call | tf_op jit(solution)/shard_map/pallas_call | solution.py:626

commit v4 on v3

--- a/solution.py
+++ b/solution.py
@@ -10,6 +10,7 @@
 
 MESH = pl.DeviceIdType.MESH
 VM = pl.BlockSpec(memory_space=pltpu.VMEM)
+SM = pl.BlockSpec(memory_space=pltpu.SMEM)
 ANY = pl.BlockSpec(memory_space=pl.ANY)
 F32, BF16 = jnp.float32, jnp.bfloat16
 YS, ZS, XS = 4, 16, 4
@@ -24,7 +25,6 @@
     "wk": ((D, D), BF16),
     "proj": ((H, E, E), F32),
     "wv": ((D, D), BF16),
-    "live": ((1,), jnp.int32),
     "wq": ((D, D), BF16),
     "cot": ((T, N, D), BF16),
     "down": ((F, D), BF16),
@@ -93,7 +93,7 @@
         self.buf_c, self.acc_c = r["bufc" + tag], r["accc" + tag]
         self.buf_y, self.acc_y, self.buf_z = r["bufy" + tag], r["accy" + tag], r["bufz" + tag]
         self.sc, self.rc, self.sy, self.ry = r["sc" + tag], r["rc" + tag], r["sy" + tag], r["ry" + tag]
-        self.sz, self.rz = r["sz" + tag], r["rz" + tag]
+        self.sz, self.rz, self.ryd = r["sz" + tag], r["rz" + tag], r["ryd" + tag]
 
     def core_down(self, k):
         chunk = lax.rem(self.pos[1] + k, YS)
@@ -101,12 +101,14 @@
             self.x.at[1 - self.pos[3], chunk], self.buf_c.at[chunk], self.sc.at[0, k], self.rc.at[0, k], self.peers["c"]
         )
 
-    def y_down(self, d):
+    def y_down(self, d, tiles):
         chunk = lax.rem(self.pos[1] + d, YS)
-        return send(
-            self.acc_c.at[chunk], self.buf_y.at[d - 1], self.sy.at[0, d - 1], self.ry.at[0, d - 1],
-            self.peers["y"][d - 1],
-        )
+        if tiles is None:
+            source, target, arrived = self.acc_c.at[chunk], self.buf_y.at[d - 1], self.ryd.at[d - 1, 0]
+        else:
+            source, target = self.acc_c.at[chunk, tiles], self.buf_y.at[d - 1, tiles]
+            arrived = self.ryd.at[d - 1, tiles]
+        return send(source, target, self.sy.at[0, d - 1], arrived, self.peers["y"][d - 1])
 
     def z_down(self, d, slot):
         return send(
@@ -129,25 +131,32 @@
             self.core_down(k).start()
 
     def start_y(self):
-        _, y, _, c = self.pos
+        _, y, z, c = self.pos
         for k in FAR_4 + (0,):
             self.core_down(k).wait()
             chunk = lax.rem(y + k, YS)
             self.acc_c[chunk] = self.x[c, chunk] + self.buf_c[chunk]
             if k:
-                self.y_down(k).start()
+                for d in FAR_16 + (0,):
+                    tile = lax.rem(z + d, ZS)
+
+                    @pl.when(tile < TILES)
+                    def _():
+                        self.y_down(k, tile).start()
 
     def start_z(self):
         _, y, z, _ = self.pos
-        for d in range(1, YS):
-            self.y_down(d).wait()
-        self.acc_y[...] = self.acc_c[y] + self.buf_y[0] + self.buf_y[1] + self.buf_y[2]
-        for d in FAR_16:
-            other = lax.rem(z + d, ZS)
-
-            @pl.when(other < TILES)
+        for d in FAR_16 + (0,):
+            tile = lax.rem(z + d, ZS)
+
+            @pl.when(tile < TILES)
             def _():
-                self.z_down(d, other).start()
+                for k in range(1, YS):
+                    self.y_down(k, tile).wait_recv()
+                parts = [self.buf_y[k, tile] for k in range(YS - 1)]
+                self.acc_y[tile] = self.acc_c[y, tile] + parts[0] + parts[1] + parts[2]
+                if d:
+                    self.z_down(d, tile).start()
 
     def start_z_back(self):
         _, y, z, c = self.pos
@@ -203,6 +212,7 @@
 
         for d in range(1, YS):
             self.y_up(d, self.out.at[c, y]).wait_send()
+            self.y_down(d, None).wait_send()
         for k in range(YS):
             self.core_up(k, lax.rem(y + YS - k, YS)).wait_send()
 
@@ -283,11 +293,11 @@
             self.ref("send" + name).at[chunk], self.ref("got" + name).at[chunk], *self.sems("1", half, k), self.peers["c"]
         )
 
-    def second_copy(self, half, d):
-        name = "xy"[half]
+    def second_copy(self, half, d, k):
+        name, part = "xy"[half], self.chunk(1 - half, k)
         return send(
-            self.ref("own" + name).at[self.chunk(half, d)], self.ref("b" + name).at[d - 1],
-            *self.sems("2", half, d - 1), self.peers[name][d - 1],
+            self.ref("own" + name).at[self.chunk(half, d), part], self.ref("b" + name).at[d - 1, part],
+            self.ref("s2").at[half, d - 1, k], self.ref("r2").at[half, d - 1, k], self.peers[name][d - 1],
         )
 
     def third_copy(self, half, d):
@@ -316,17 +326,20 @@
                 chunk = self.chunk(half, k)
                 own[chunk] = own[chunk] + got[chunk]
                 if k:
-                    self.second_copy(half, k).start()
+                    for part in FAR_4 + (0,):
+                        self.second_copy(half, k, part).start()
 
     def start_third(self):
-        for half in range(2):
-            name = "xy"[half]
-            for d in range(1, 4):
-                self.second_copy(half, d).wait()
-            got = self.ref("b" + name)
-            self.ref("c" + name)[...] = self.ref("own" + name)[self.pos[half]] + got[0] + got[1] + got[2]
-            for d in FAR_4:
-                self.third_copy(half, d).start()
+        for k in FAR_4 + (0,):
+            for half in range(2):
+                name, part = "xy"[half], self.chunk(1 - half, k)
+                for d in range(1, 4):
+                    self.second_copy(half, d, k).wait()
+                got, own = self.ref("b" + name), self.ref("own" + name)
+                total = own[self.pos[half], part] + got[0, part] + got[1, part] + got[2, part]
+                self.ref("c" + name)[part] = total
+                if k:
+                    self.third_copy(half, k).start()
 
     def start_last(self):
         zs = self.ref("zs")
@@ -360,6 +373,7 @@
         "rc" + tag: dma((2, YS)),
         "sy" + tag: dma((2, YS - 1)),
         "ry" + tag: dma((2, YS - 1)),
+        "ryd" + tag: dma((YS - 1, TILES)),
         "sz" + tag: dma((2, ZS - 1)),
         "rz" + tag: dma((2, ZS - 1)),
     }
@@ -376,9 +390,9 @@
         names["d" + axis + tag] = pltpu.VMEM((3, 32, 128), F32)
     names["zs" + tag] = pltpu.VMEM((ZS, 4, 128), F32)
     names["zb" + tag] = pltpu.VMEM((ZS - 1, 4, 128), F32)
-    for k in ("1", "2", "3"):
-        names["s" + k + tag] = dma((2, 4))
-        names["r" + k + tag] = dma((2, 4))
+    for k, shape in (("1", (2, 4)), ("2", (2, 3, 4)), ("3", (2, 3))):
+        names["s" + k + tag] = dma(shape)
+        names["r" + k + tag] = dma(shape)
     names["s4" + tag] = dma((ZS - 1,))
     names["r4" + tag] = dma((ZS - 1,))
     return names
@@ -401,18 +415,18 @@
     for tag in ("_q", "_k", "_v"):
         names.update(scatter_scratch(tag))
     for n, (shape, kind) in STAGED.items():
-        names["in_" + n] = pltpu.SMEM(shape, kind) if n == "live" else pltpu.VMEM(shape, kind)
+        names["in_" + n] = pltpu.VMEM(shape, kind)
     names["fetch"] = pltpu.SemaphoreType.DMA((len(STAGED),))
     return names
 
 
 def kernel(
-    scale, x_hbm, cot_hbm, wq_hbm, wk_hbm, wv_hbm, up_hbm, down_hbm, proj_hbm, live_hbm,
+    scale, x_hbm, cot_hbm, wq_hbm, wk_hbm, wv_hbm, up_hbm, down_hbm, proj_hbm, live_ref,
     gin_ref, oq_ref, ok_ref, ov_ref, *rest,
 ):
     r = dict(zip(scratch().keys(), rest))
     sources = dict(
-        x=x_hbm, cot=cot_hbm, wq=wq_hbm, wk=wk_hbm, wv=wv_hbm, up=up_hbm, down=down_hbm, proj=proj_hbm, live=live_hbm
+        x=x_hbm, cot=cot_hbm, wq=wq_hbm, wk=wk_hbm, wv=wv_hbm, up=up_hbm, down=down_hbm, proj=proj_hbm
     )
     fetches = {
         n: pltpu.make_async_copy(sources[n], r["in_" + n], r["fetch"].at[i]) for i, n in enumerate(STAGED)
@@ -466,7 +480,7 @@
         return (back * FACTOR).astype(BF16)
 
     r["vh"][...], r["vl"][...] = split(dot(rows, fetched("wv")[...]))
-    valid = row_id < fetched("live")[0]
+    valid = row_id < live_ref[0]
     for q in range(2):
         fk = jnp.where(valid, features(r["uk"], q), 0.0)
         r["fk"][:, quads[q]] = fk
@@ -563,10 +577,9 @@
     job_q.start_second()
     r["gin"][...] = dot_nt(r["gq"][...], wq_ref[...])
     second.start_z_back()
+    second.start_y_back()
     job_q.start_third()
-    second.start_y_back()
     second.start_core_back()
-    job_q.start_last()
     second.finish()
 
     for t in range(T):
@@ -577,6 +590,7 @@
             r["gv"][here] = dot3(dot, (r["fkh"][here], r["fkl"][here]), blocks).astype(BF16)
     job_v.put("send", dot(r["turn"][1 - c], r["gv"][...]))
     job_v.start_core()
+    job_q.start_last()
     for t in range(T):
         for q in range(2):
             here = moments[t], quads[q]
@@ -605,10 +619,8 @@
 
 
 def hand_on(*refs):
-    ins, outs, sem = refs[:4], refs[4:8], refs[8]
-    copies = [pltpu.make_async_copy(a, b, sem.at[i]) for i, (a, b) in enumerate(zip(ins, outs))]
-    start(copies)
-    wait(copies)
+    for source, target in zip(refs[:4], refs[4:]):
+        target[...] = source[...]
 
 
 def shards(inputs, cotangent, w_query, w_key, w_value, w_up, w_down, feature_proj, live_count):
@@ -618,7 +630,7 @@
     results = pl.pallas_call(
         functools.partial(kernel, 1.0 / math.sqrt(total_rows)),
         out_shape=shapes,
-        in_specs=[ANY] * 8 + [pl.BlockSpec(memory_space=pltpu.HBM)],
+        in_specs=[ANY] * 8 + [SM],
         out_specs=(VM,) * 4,
         scratch_shapes=list(scratch().values()),
         compiler_params=pltpu.CompilerParams(collective_id=0, has_side_effects=True, vmem_limit_bytes=56 << 20),
@@ -626,9 +638,8 @@
     return pl.pallas_call(
         hand_on,
         out_shape=shapes,
-        in_specs=[ANY] * 4,
-        out_specs=(ANY,) * 4,
-        scratch_shapes=[pltpu.SemaphoreType.DMA((4,))],
+        in_specs=[VM] * 4,
+        out_specs=(VM,) * 4,
     )(*results)
 
 

time: 101 us -> 94.2 us (0.933)
  Pallas kernels: 99.7 us -> 92.7 us
    pallas_call x1, Pallas kernels: 7.28 us -> 1.63 us  [shards(): pl.pallas_call(hand_on, out_shape=shapes, in_specs=[VM] * 4, out_specs=(V...]
    pallas_call x1, Pallas kernels: 92.4 us -> 91.1 us  [shards(): pl.pallas_call(functools.partial(kernel, 1.0 / math.sqrt(total_rows)), ou...]
where the time goes in v4:
time: 94.2 us; the launch traced here: 94 us
  Pallas kernels  92.7 us (98%)
  between operations  1.29 us (1%)
    pallas_call x1, Pallas kernels, shards(): pl.pallas_call(functools.partial(kernel, 1.0 / math.sqrt(total_rows)), ou...  91.1 us

profile of v4, /device:TPU:1, one launch (start us, length us, event | category | flops | bytes accessed | tf_op | source)
XLA Modules:
  0.0 94.0 jit_solution(10137959230093505718)
XLA Ops:
  1.3 91.1 %shard_map.120 = (bf16[3,64,512]{2,1,0:T(8,128)(2,1)}, f32[4,128]{1,0:T(4,128)}, f32[4,128]{1,0:T(4,128)}, f32[4,128]{1,0:T(4,128)}) custom-call(bf16[3,64,512]{2,1,0:T(8,128)(2,1)} %x_hbm.1, bf16[3,64,512]{2,1,0:T(8,128)(2,1)} %cot_hbm.1, bf16[512,512]{1,0:T(8,128)(2,1)} %wq_hbm.1, bf16[512,512]{1,0:T(8,128)(2,1)} %wk_hbm.1, bf16[512,512]{1,0:T(8,128)(2,1)} %wv_hbm.1, ...), custom_call_target="tpu_custom_call" | custom-call | tf_op jit(solution)/shard_map/pallas_call | solution.py:630
  92.4 1.6 %shard_map.121 = (bf16[3,64,512]{2,1,0:T(8,128)(2,1)}, f32[4,128]{1,0:T(4,128)}, f32[4,128]{1,0:T(4,128)}, f32[4,128]{1,0:T(4,128)}) custom-call(bf16[3,64,512]{2,1,0:T(8,128)(2,1)} %get-tuple-element.8.refs_0_, f32[4,128]{1,0:T(4,128)} %get-tuple-element.9.refs_1_, f32[4,128]{1,0:T(4,128)} %get-tuple-element.10.refs_2_, f32[4,128]{1,0:T(4,128)} %get-tuple-element.11.refs_3_), custom_call_target="tpu_custom_call" | custom-call | tf_op jit(solution)/shard_map/pallas_call | solution.py:638

commit v5 on v4

--- a/solution.py
+++ b/solution.py
@@ -54,6 +54,14 @@
         copy.wait()
 
 
+def arrival(ref, landed, sent, peer):
+    send(ref, ref, sent, landed, peer).wait_recv()
+
+
+def departure(ref, sent, landed, peer):
+    send(ref, ref, sent, landed, peer).wait_send()
+
+
 def dot(a, b):
     return lax.dot_general(a, b, (((1,), (0,)), ((), ())), preferred_element_type=F32)
 
@@ -92,39 +100,32 @@
         self.x, self.out = r["x" + tag], r["out" + tag]
         self.buf_c, self.acc_c = r["bufc" + tag], r["accc" + tag]
         self.buf_y, self.acc_y, self.buf_z = r["bufy" + tag], r["accy" + tag], r["bufz" + tag]
-        self.sc, self.rc, self.sy, self.ry = r["sc" + tag], r["rc" + tag], r["sy" + tag], r["ry" + tag]
-        self.sz, self.rz, self.ryd = r["sz" + tag], r["rz" + tag], r["ryd" + tag]
+        self.sent, self.core_in, self.y_in = r["sent" + tag], r["corein" + tag], r["yin" + tag]
+        self.z_in, self.z_out, self.y_out, self.core_out = r["zin" + tag], r["zout" + tag], r["yout" + tag], r["coreout" + tag]
 
     def core_down(self, k):
         chunk = lax.rem(self.pos[1] + k, YS)
-        return send(
-            self.x.at[1 - self.pos[3], chunk], self.buf_c.at[chunk], self.sc.at[0, k], self.rc.at[0, k], self.peers["c"]
-        )
-
-    def y_down(self, d, tiles):
+        source = self.x.at[1 - self.pos[3], chunk]
+        return send(source, self.buf_c.at[chunk], self.sent.at[0], self.core_in.at[k], self.peers["c"])
+
+    def y_down(self, d, tile):
         chunk = lax.rem(self.pos[1] + d, YS)
-        if tiles is None:
-            source, target, arrived = self.acc_c.at[chunk], self.buf_y.at[d - 1], self.ryd.at[d - 1, 0]
-        else:
-            source, target = self.acc_c.at[chunk, tiles], self.buf_y.at[d - 1, tiles]
-            arrived = self.ryd.at[d - 1, tiles]
-        return send(source, target, self.sy.at[0, d - 1], arrived, self.peers["y"][d - 1])
-
-    def z_down(self, d, slot):
-        return send(
-            self.acc_y.at[slot], self.buf_z.at[d - 1], self.sz.at[0, d - 1], self.rz.at[0, d - 1], self.peers["z"][d - 1]
-        )
-
-    def z_up(self, d, slot):
-        piece = self.out.at[self.pos[3], self.pos[1], slot]
-        return send(piece, piece, self.sz.at[1, d - 1], self.rz.at[1, d - 1], self.peers["z"][d - 1])
+        target = self.buf_y.at[tile, d - 1]
+        return send(self.acc_c.at[chunk, tile], target, self.sent.at[1], self.y_in.at[tile], self.peers["y"][d - 1])
+
+    def z_down(self, d, tile):
+        return send(self.acc_y.at[tile], self.buf_z.at[d - 1], self.sent.at[2], self.z_in.at[0], self.peers["z"][d - 1])
+
+    def z_up(self, d, tile):
+        piece = self.out.at[self.pos[3], self.pos[1], tile]
+        return send(piece, piece, self.sent.at[3], self.z_out.at[tile], self.peers["z"][d - 1])
 
     def y_up(self, d, piece):
-        return send(piece, piece, self.sy.at[1, d - 1], self.ry.at[1, d - 1], self.peers["y"][d - 1])
-
-    def core_up(self, k, group):
+        return send(piece, piece, self.sent.at[4], self.y_out.at[d - 1], self.peers["y"][d - 1])
+
+    def core_up(self, group):
         piece = self.out.at[self.pos[3], group]
-        return send(piece, piece, self.sc.at[1, k], self.rc.at[1, k], self.peers["c"])
+        return send(piece, piece, self.sent.at[5], self.core_out.at[0], self.peers["c"])
 
     def start_core(self):
         for k in FAR_4 + (0,):
@@ -133,7 +134,7 @@
     def start_y(self):
         _, y, z, c = self.pos
         for k in FAR_4 + (0,):
-            self.core_down(k).wait()
+            self.core_down(k).wait_recv()
             chunk = lax.rem(y + k, YS)
             self.acc_c[chunk] = self.x[c, chunk] + self.buf_c[chunk]
             if k:
@@ -151,10 +152,9 @@
 
             @pl.when(tile < TILES)
             def _():
-                for k in range(1, YS):
-                    self.y_down(k, tile).wait_recv()
-                parts = [self.buf_y[k, tile] for k in range(YS - 1)]
-                self.acc_y[tile] = self.acc_c[y, tile] + parts[0] + parts[1] + parts[2]
+                landed = self.buf_y.at[tile]
+                arrival(landed, self.y_in.at[tile], self.sent.at[1], self.peers["c"])
+                self.acc_y[tile] = self.acc_c[y, tile] + landed[0] + landed[1] + landed[2]
                 if d:
                     self.z_down(d, tile).start()
 
@@ -163,8 +163,7 @@
 
         @pl.when(z < TILES)
         def _():
-            for d in range(1, ZS):
-                self.z_down(d, 0).wait_recv()
+            arrival(self.buf_z, self.z_in.at[0], self.sent.at[2], self.peers["c"])
             self.out[c, y, z] = self.acc_y[z] + sum(self.buf_z[d - 1] for d in range(1, ZS))
             for d in FAR_16:
                 self.z_up(d, z).start()
@@ -184,37 +183,30 @@
 
     def start_core_back(self):
         _, y, _, c = self.pos
-        self.core_up(0, y).start()
+        self.core_up(y).start()
         for d in (1, 3, 2):
             group = lax.rem(y + YS - d, YS)
             self.y_up(d, self.out.at[c, group]).wait_recv()
-            self.core_up(d, group).start()
+            self.core_up(group).start()
 
     def finish(self):
-        for k in range(YS):
-            group = lax.rem(self.pos[1] + YS - k, YS)
-            piece = self.out.at[1 - self.pos[3], group]
-            send(piece, piece, self.sc.at[1, k], self.rc.at[1, k], self.peers["c"]).wait_recv()
+        arrival(self.out.at[1 - self.pos[3]], self.core_out.at[0], self.sent.at[5], self.peers["c"])
 
     def drain(self):
-        _, y, z, c = self.pos
-        for d in range(1, ZS):
-            other = lax.rem(z + d, ZS)
-
-            @pl.when(other < TILES)
-            def _():
-                self.z_down(d, other).wait_send()
+        z, peer = self.pos[2], self.peers["c"]
+        departure(self.buf_c, self.sent.at[0], self.core_in.at[0], peer)
+        departure(self.buf_y, self.sent.at[1], self.y_in.at[0], peer)
+        departure(self.buf_y, self.sent.at[4], self.y_in.at[0], peer)
+        departure(self.buf_c, self.sent.at[5], self.core_in.at[0], peer)
 
         @pl.when(z < TILES)
         def _():
-            for d in range(1, ZS):
-                self.z_up(d, z).wait_send()
-
-        for d in range(1, YS):
-            self.y_up(d, self.out.at[c, y]).wait_send()
-            self.y_down(d, None).wait_send()
-        for k in range(YS):
-            self.core_up(k, lax.rem(y + YS - k, YS)).wait_send()
+            departure(self.acc_y.at[pl.ds(0, TILES - 1)], self.sent.at[2], self.z_in.at[0], peer)
+            departure(self.buf_z, self.sent.at[3], self.z_in.at[0], peer)
+
+        @pl.when(z >= TILES)
+        def _():
+            departure(self.acc_y, self.sent.at[2], self.z_in.at[0], peer)
 
 
 def tile_place(tile):
@@ -281,36 +273,37 @@
                 xf[x, y] = block[0:32]
                 yf[y, x] = block[32:64]
 
-    def sems(self, phase, half, k):
-        return self.ref("s" + phase).at[half, k], self.ref("r" + phase).at[half, k]
-
     def chunk(self, half, k):
         return lax.rem(self.pos[half] + k, 4)
+
+    def sent(self, phase, half):
+        return self.ref("sent").at[2 * phase + half]
 
     def core_copy(self, half, k):
         name, chunk = "xy"[half], self.chunk(half, k)
         return send(
-            self.ref("send" + name).at[chunk], self.ref("got" + name).at[chunk], *self.sems("1", half, k), self.peers["c"]
+            self.ref("send" + name).at[chunk], self.ref("got" + name).at[chunk], self.sent(0, half),
+            self.ref("in1").at[half, k], self.peers["c"],
         )
 
     def second_copy(self, half, d, k):
         name, part = "xy"[half], self.chunk(1 - half, k)
         return send(
-            self.ref("own" + name).at[self.chunk(half, d), part], self.ref("b" + name).at[d - 1, part],
-            self.ref("s2").at[half, d - 1, k], self.ref("r2").at[half, d - 1, k], self.peers[name][d - 1],
+            self.ref("own" + name).at[self.chunk(half, d), part], self.ref("b" + name).at[part, d - 1],
+            self.sent(1, half), self.ref("in2").at[half, k], self.peers[name][d - 1],
         )
 
     def third_copy(self, half, d):
         name, other = "xy"[half], "yx"[half]
         return send(
             self.ref("c" + name).at[self.chunk(1 - half, d)], self.ref("d" + name).at[d - 1],
-            *self.sems("3", half, d - 1), self.peers[other][d - 1],
+            self.sent(2, half), self.ref("in3").at[half], self.peers[other][d - 1],
         )
 
     def last_copy(self, d):
         return send(
             self.ref("zs").at[lax.rem(self.pos[2] + d, ZS)], self.ref("zb").at[d - 1],
-            self.ref("s4").at[d - 1], self.ref("r4").at[d - 1], self.peers["z"][d - 1],
+            self.sent(3, 0), self.ref("in3").at[2], self.peers["z"][d - 1],
         )
 
     def start_core(self):
@@ -321,7 +314,7 @@
     def start_second(self):
         for k in FAR_4 + (0,):
             for half in range(2):
-                self.core_copy(half, k).wait()
+                self.core_copy(half, k).wait_recv()
                 own, got = self.ref("own" + "xy"[half]), self.ref("got" + "xy"[half])
                 chunk = self.chunk(half, k)
                 own[chunk] = own[chunk] + got[chunk]
@@ -333,30 +326,34 @@
         for k in FAR_4 + (0,):
             for half in range(2):
                 name, part = "xy"[half], self.chunk(1 - half, k)
-                for d in range(1, 4):
-                    self.second_copy(half, d, k).wait()
-                got, own = self.ref("b" + name), self.ref("own" + name)
-                total = own[self.pos[half], part] + got[0, part] + got[1, part] + got[2, part]
-                self.ref("c" + name)[part] = total
+                landed, own = self.ref("b" + name).at[part], self.ref("own" + name)
+                arrival(landed, self.ref("in2").at[half, k], self.sent(1, half), self.peers["c"])
+                self.ref("c" + name)[part] = own[self.pos[half], part] + landed[0] + landed[1] + landed[2]
                 if k:
                     self.third_copy(half, k).start()
 
     def start_last(self):
         zs = self.ref("zs")
         for half in range(2):
-            for d in range(1, 4):
-                self.third_copy(half, d).wait()
-            got = self.ref("d" + "xy"[half])
-            total = self.ref("c" + "xy"[half])[self.pos[1 - half]] + got[0] + got[1] + got[2]
+            landed = self.ref("d" + "xy"[half])
+            arrival(landed, self.ref("in3").at[half], self.sent(2, half), self.peers["c"])
+            total = self.ref("c" + "xy"[half])[self.pos[1 - half]] + landed[0] + landed[1] + landed[2]
             zs[8 * half : 8 * half + 8] = total.reshape(8, 4, 128)
         for d in FAR_16:
             self.last_copy(d).start()
 
     def finish(self, out, scale):
-        for d in range(1, ZS):
-            self.last_copy(d).wait()
         zb = self.ref("zb")
+        arrival(zb, self.ref("in3").at[2], self.sent(3, 0), self.peers["c"])
         out[...] = (self.ref("zs")[self.pos[2]] + sum(zb[d - 1] for d in range(1, ZS))) * scale
+
+    def drain(self):
+        spare = self.ref("in3").at[0]
+        for half, name in enumerate("xy"):
+            departure(self.ref("send" + name), self.sent(0, half), spare, self.peers["c"])
+            departure(self.ref("b" + name), self.sent(1, half), spare, self.peers["c"])
+            departure(self.ref("d" + name), self.sent(2, half), spare, self.peers["c"])
+        departure(self.ref("zb"), self.sent(3, 0), spare, self.peers["c"])
 
 
 def reduce_scratch(tag):
@@ -366,16 +363,16 @@
         "out" + tag: pltpu.VMEM((2, YS, TILES, 8, 128), F32),
         "bufc" + tag: pltpu.VMEM((YS, TILES, 8, 128), F32),
         "accc" + tag: pltpu.VMEM((YS, TILES, 8, 128), F32),
-        "bufy" + tag: pltpu.VMEM((YS - 1, TILES, 8, 128), F32),
+        "bufy" + tag: pltpu.VMEM((TILES, YS - 1, 8, 128), F32),
         "accy" + tag: pltpu.VMEM((TILES, 8, 128), F32),
         "bufz" + tag: pltpu.VMEM((ZS - 1, 8, 128), F32),
-        "sc" + tag: dma((2, YS)),
-        "rc" + tag: dma((2, YS)),
-        "sy" + tag: dma((2, YS - 1)),
-        "ry" + tag: dma((2, YS - 1)),
-        "ryd" + tag: dma((YS - 1, TILES)),
-        "sz" + tag: dma((2, ZS - 1)),
-        "rz" + tag: dma((2, ZS - 1)),
+        "sent" + tag: dma((6,)),
+        "corein" + tag: dma((YS,)),
+        "yin" + tag: dma((TILES,)),
+        "zin" + tag: dma((1,)),
+        "zout" + tag: dma((TILES,)),
+        "yout" + tag: dma((YS - 1,)),
+        "coreout" + tag: dma((1,)),
     }
 
 
@@ -385,16 +382,15 @@
     for axis in ("x", "y"):
         for kind in ("send", "got", "own"):
             names[kind + axis + tag] = pltpu.VMEM((4, 4, 32, 128), F32)
-        names["b" + axis + tag] = pltpu.VMEM((3, 4, 32, 128), F32)
+        names["b" + axis + tag] = pltpu.VMEM((4, 3, 32, 128), F32)
         names["c" + axis + tag] = pltpu.VMEM((4, 32, 128), F32)
         names["d" + axis + tag] = pltpu.VMEM((3, 32, 128), F32)
     names["zs" + tag] = pltpu.VMEM((ZS, 4, 128), F32)
     names["zb" + tag] = pltpu.VMEM((ZS - 1, 4, 128), F32)
-    for k, shape in (("1", (2, 4)), ("2", (2, 3, 4)), ("3", (2, 3))):
-        names["s" + k + tag] = dma(shape)
-        names["r" + k + tag] = dma(shape)
-    names["s4" + tag] = dma((ZS - 1,))
-    names["r4" + tag] = dma((ZS - 1,))
+    names["sent" + tag] = dma((7,))
+    names["in1" + tag] = dma((2, 4))
+    names["in2" + tag] = dma((2, 4))
+    names["in3" + tag] = dma((3,))
     return names
 
 
@@ -614,8 +610,8 @@
     job_q.finish(oq_ref, scale)
     job_v.finish(ov_ref, scale)
     job_k.finish(ok_ref, scale)
-    first.drain()
-    second.drain()
+    for job in (first, second, job_q, job_k, job_v):
+        job.drain()
 
 
 def hand_on(*refs):

time: 94.2 us -> 90 us (0.955)
  Pallas kernels: 92.7 us -> 88.6 us
    pallas_call x1, Pallas kernels: 91.1 us -> 86.9 us  [shards(): pl.pallas_call(functools.partial(kernel, 1.0 / math.sqrt(total_rows)), ou...]
where the time goes in v5:
time: 90 us; the launch traced here: 89.9 us
  Pallas kernels  88.6 us (98%)
  between operations  1.29 us (1%)
    pallas_call x1, Pallas kernels, shards(): pl.pallas_call(functools.partial(kernel, 1.0 / math.sqrt(total_rows)), ou...  86.9 us

profile of v5, /device:TPU:1, one launch (start us, length us, event | category | flops | bytes accessed | tf_op | source)
XLA Modules:
  0.0 89.9 jit_solution(5577821026055501219)
XLA Ops:
  1.3 86.9 %shard_map.120 = (bf16[3,64,512]{2,1,0:T(8,128)(2,1)}, f32[4,128]{1,0:T(4,128)}, f32[4,128]{1,0:T(4,128)}, f32[4,128]{1,0:T(4,128)}) custom-call(bf16[3,64,512]{2,1,0:T(8,128)(2,1)} %x_hbm.1, bf16[3,64,512]{2,1,0:T(8,128)(2,1)} %cot_hbm.1, bf16[512,512]{1,0:T(8,128)(2,1)} %wq_hbm.1, bf16[512,512]{1,0:T(8,128)(2,1)} %wk_hbm.1, bf16[512,512]{1,0:T(8,128)(2,1)} %wv_hbm.1, ...), custom_call_target="tpu_custom_call" | custom-call | tf_op jit(solution)/shard_map/pallas_call | solution.py:626
  88.2 1.6 %shard_map.121 = (bf16[3,64,512]{2,1,0:T(8,128)(2,1)}, f32[4,128]{1,0:T(4,128)}, f32[4,128]{1,0:T(4,128)}, f32[4,128]{1,0:T(4,128)}) custom-call(bf16[3,64,512]{2,1,0:T(8,128)(2,1)} %get-tuple-element.8.refs_0_, f32[4,128]{1,0:T(4,128)} %get-tuple-element.9.refs_1_, f32[4,128]{1,0:T(4,128)} %get-tuple-element.10.refs_2_, f32[4,128]{1,0:T(4,128)} %get-tuple-element.11.refs_3_), custom_call_target="tpu_custom_call" | custom-call | tf_op jit(solution)/shard_map/pallas_call | solution.py:634

commit v6 on v5

--- a/solution.py
+++ b/solution.py
@@ -102,6 +102,7 @@
         self.buf_y, self.acc_y, self.buf_z = r["bufy" + tag], r["accy" + tag], r["bufz" + tag]
         self.sent, self.core_in, self.y_in = r["sent" + tag], r["corein" + tag], r["yin" + tag]
         self.z_in, self.z_out, self.y_out, self.core_out = r["zin" + tag], r["zout" + tag], r["yout" + tag], r["coreout" + tag]
+        self.cross = r["cross" + tag]
 
     def core_down(self, k):
         chunk = lax.rem(self.pos[1] + k, YS)
@@ -122,6 +123,9 @@
 
     def y_up(self, d, piece):
         return send(piece, piece, self.sent.at[4], self.y_out.at[d - 1], self.peers["y"][d - 1])
+
+    def cross_up(self, piece):
+        return send(piece, piece, self.sent.at[6], self.cross.at[0], self.peers["far"])
 
     def core_up(self, group):
         piece = self.out.at[self.pos[3], group]
@@ -167,6 +171,7 @@
             self.out[c, y, z] = self.acc_y[z] + sum(self.buf_z[d - 1] for d in range(1, ZS))
             for d in FAR_16:
                 self.z_up(d, z).start()
+            self.cross_up(self.out.at[c, y, z]).start()
             for d in FAR_4:
                 self.y_up(d, self.out.at[c, y, z]).start()
 
@@ -178,26 +183,32 @@
             @pl.when(source < TILES)
             def _():
                 self.z_up(d, source).wait_recv()
+                self.cross_up(self.out.at[c, y, source]).start()
                 for e in FAR_4:
                     self.y_up(e, self.out.at[c, y, source]).start()
 
     def start_core_back(self):
         _, y, _, c = self.pos
         self.core_up(y).start()
-        for d in (1, 3, 2):
+        for d in (1, 3):
             group = lax.rem(y + YS - d, YS)
             self.y_up(d, self.out.at[c, group]).wait_recv()
             self.core_up(group).start()
 
     def finish(self):
-        arrival(self.out.at[1 - self.pos[3]], self.core_out.at[0], self.sent.at[5], self.peers["c"])
+        _, y, _, c = self.pos
+        far = lax.rem(y + 2, YS)
+        self.y_up(2, self.out.at[c, far]).wait_recv()
+        arrival(self.out.at[1 - c, far], self.cross.at[0], self.sent.at[6], self.peers["far"])
+        arrival(self.buf_y, self.core_out.at[0], self.sent.at[5], self.peers["c"])
 
     def drain(self):
         z, peer = self.pos[2], self.peers["c"]
         departure(self.buf_c, self.sent.at[0], self.core_in.at[0], peer)
         departure(self.buf_y, self.sent.at[1], self.y_in.at[0], peer)
         departure(self.buf_y, self.sent.at[4], self.y_in.at[0], peer)
-        departure(self.buf_c, self.sent.at[5], self.core_in.at[0], peer)
+        departure(self.buf_y, self.sent.at[5], self.core_in.at[0], peer)
+        departure(self.acc_y, self.sent.at[6], self.core_in.at[0], peer)
 
         @pl.when(z < TILES)
         def _():
@@ -283,14 +294,14 @@
         name, chunk = "xy"[half], self.chunk(half, k)
         return send(
             self.ref("send" + name).at[chunk], self.ref("got" + name).at[chunk], self.sent(0, half),
-            self.ref("in1").at[half, k], self.peers["c"],
+            self.ref("in1").at[k], self.peers["c"],
         )
 
     def second_copy(self, half, d, k):
         name, part = "xy"[half], self.chunk(1 - half, k)
         return send(
             self.ref("own" + name).at[self.chunk(half, d), part], self.ref("b" + name).at[part, d - 1],
-            self.sent(1, half), self.ref("in2").at[half, k], self.peers[name][d - 1],
+            self.sent(1, half), self.ref("in2").at[k], self.peers[name][d - 1],
         )
 
     def third_copy(self, half, d):
@@ -313,8 +324,8 @@
 
     def start_second(self):
         for k in FAR_4 + (0,):
+            arrival(self.ref("gotx").at[pl.ds(0, 2)], self.ref("in1").at[k], self.sent(0, 0), self.peers["c"])
             for half in range(2):
-                self.core_copy(half, k).wait_recv()
                 own, got = self.ref("own" + "xy"[half]), self.ref("got" + "xy"[half])
                 chunk = self.chunk(half, k)
                 own[chunk] = own[chunk] + got[chunk]
@@ -324,10 +335,10 @@
 
     def start_third(self):
         for k in FAR_4 + (0,):
+            arrival(self.ref("bx").at[pl.ds(0, 2)], self.ref("in2").at[k], self.sent(1, 0), self.peers["c"])
             for half in range(2):
                 name, part = "xy"[half], self.chunk(1 - half, k)
                 landed, own = self.ref("b" + name).at[part], self.ref("own" + name)
-                arrival(landed, self.ref("in2").at[half, k], self.sent(1, half), self.peers["c"])
                 self.ref("c" + name)[part] = own[self.pos[half], part] + landed[0] + landed[1] + landed[2]
                 if k:
                     self.third_copy(half, k).start()
@@ -366,7 +377,8 @@
         "bufy" + tag: pltpu.VMEM((TILES, YS - 1, 8, 128), F32),
         "accy" + tag: pltpu.VMEM((TILES, 8, 128), F32),
         "bufz" + tag: pltpu.VMEM((ZS - 1, 8, 128), F32),
-        "sent" + tag: dma((6,)),
+        "sent" + tag: dma((7,)),
+        "cross" + tag: dma((1,)),
         "corein" + tag: dma((YS,)),
         "yin" + tag: dma((TILES,)),
         "zin" + tag: dma((1,)),
@@ -388,8 +400,8 @@
     names["zs" + tag] = pltpu.VMEM((ZS, 4, 128), F32)
     names["zb" + tag] = pltpu.VMEM((ZS - 1, 4, 128), F32)
     names["sent" + tag] = dma((7,))
-    names["in1" + tag] = dma((2, 4))
-    names["in2" + tag] = dma((2, 4))
+    names["in1" + tag] = dma((4,))
+    names["in2" + tag] = dma((4,))
     names["in3" + tag] = dma((3,))
     return names
 
@@ -412,7 +424,8 @@
         names.update(scatter_scratch(tag))
     for n, (shape, kind) in STAGED.items():
         names["in_" + n] = pltpu.VMEM(shape, kind)
-    names["fetch"] = pltpu.SemaphoreType.DMA((len(STAGED),))
+    names["fetch"] = pltpu.SemaphoreType.DMA((len(STAGED) + 1,))
+    names["gout"] = pltpu.VMEM((T, N, D), BF16)
     return names
 
 
@@ -427,7 +440,7 @@
     fetches = {
         n: pltpu.make_async_copy(sources[n], r["in_" + n], r["fetch"].at[i]) for i, n in enumerate(STAGED)
     }
-    start(fetches.values())
+    start([fetches[n] for n in ("x", "wk", "proj", "wv")])
 
     def fetched(n):
         fetches[n].wait()
@@ -442,7 +455,8 @@
         "x": [at(lax.rem(x + d, XS), y, z, c) for d in range(1, XS)],
         "z": [at(x, y, lax.rem(z + d, ZS), c) for d in range(1, ZS)],
     }
-    everyone = [peers["c"]] + peers["y"] + peers["x"] + peers["z"]
+    peers["far"] = at(x, lax.rem(y + 2, YS), z, 1 - c)
+    everyone = [peers["c"], peers["far"]] + peers["y"] + peers["x"] + peers["z"]
     barrier = pltpu.get_barrier_semaphore()
     for target in everyone:
         pl.semaphore_signal(barrier, inc=1, device_id=target, device_id_type=MESH)
@@ -457,6 +471,7 @@
     zero = jnp.zeros((E, E), F32)
     rows = fetched("x")[...].reshape(ROWS, D)
     r["uk"][...] = dot(rows, fetched("wk")[...]) * FACTOR
+    start([fetches[n] for n in ("wq", "cot", "down", "up")])
     proj_ref = fetched("proj")
     for q in range(2):
         lines = []
@@ -586,7 +601,6 @@
             r["gv"][here] = dot3(dot, (r["fkh"][here], r["fkl"][here]), blocks).astype(BF16)
     job_v.put("send", dot(r["turn"][1 - c], r["gv"][...]))
     job_v.start_core()
-    job_q.start_last()
     for t in range(T):
         for q in range(2):
             here = moments[t], quads[q]
@@ -597,12 +611,15 @@
         r["gk"][:, quads[q]] = feature_back(r["wtd"][:, quads[q]], r["uk"][:, quads[q]], q)
     job_k.put("send", dot(r["turn"][1 - c], r["gk"][...]))
     job_k.start_core()
+    job_q.start_last()
     job_v.put("own", dot(r["turn"][c], r["gv"][...]))
     job_v.start_second()
     job_k.put("own", dot(r["turn"][c], r["gk"][...]))
     job_k.start_second()
     total = r["gin"][...] + dot_nt(r["gk"][...], r["in_wk"][...]) + dot_nt(r["gv"][...], r["in_wv"][...])
-    gin_ref[...] = total.astype(BF16).reshape(T, N, D)
+    r["gout"][...] = total.astype(BF16).reshape(T, N, D)
+    leave = pltpu.make_async_copy(r["gout"], gin_ref, r["fetch"].at[len(STAGED)])
+    leave.start()
     job_v.start_third()
     job_k.start_third()
     job_v.start_last()
@@ -612,6 +629,7 @@
     job_k.finish(ok_ref, scale)
     for job in (first, second, job_q, job_k, job_v):
         job.drain()
+    leave.wait()
 
 
 def hand_on(*refs):
@@ -627,7 +645,7 @@
         functools.partial(kernel, 1.0 / math.sqrt(total_rows)),
         out_shape=shapes,
         in_specs=[ANY] * 8 + [SM],
-        out_specs=(VM,) * 4,
+        out_specs=(ANY, VM, VM, VM),
         scratch_shapes=list(scratch().values()),
         compiler_params=pltpu.CompilerParams(collective_id=0, has_side_effects=True, vmem_limit_bytes=56 << 20),
     )(inputs, cotangent, w_query, w_key, w_value, w_up, w_down, feature_proj, live_count)

time: 90 us -> 89.3 us (level)
  no operation moved by 1% of the time
where the time goes in v6:
time: 89.3 us; the launch traced here: 89.1 us
  Pallas kernels  87.9 us (98%)
  between operations  1.29 us (1%)
    pallas_call x1, Pallas kernels, shards(): pl.pallas_call(functools.partial(kernel, 1.0 / math.sqrt(total_rows)), ou...  86.2 us

profile of v6, /device:TPU:1, one launch (start us, length us, event | category | flops | bytes accessed | tf_op | source)
XLA Modules:
  0.0 89.1 jit_solution(9392812103752592281)
XLA Ops:
  1.3 86.2 %shard_map.120 = (bf16[3,64,512]{2,1,0:T(8,128)(2,1)}, f32[4,128]{1,0:T(4,128)}, f32[4,128]{1,0:T(4,128)}, f32[4,128]{1,0:T(4,128)}) custom-call(bf16[3,64,512]{2,1,0:T(8,128)(2,1)} %x_hbm.1, bf16[3,64,512]{2,1,0:T(8,128)(2,1)} %cot_hbm.1, bf16[512,512]{1,0:T(8,128)(2,1)} %wq_hbm.1, bf16[512,512]{1,0:T(8,128)(2,1)} %wk_hbm.1, bf16[512,512]{1,0:T(8,128)(2,1)} %wv_hbm.1, ...), custom_call_target="tpu_custom_call" | custom-call | tf_op jit(solution)/shard_map/pallas_call | solution.py:644
  87.5 1.6 %shard_map.121 = (bf16[3,64,512]{2,1,0:T(8,128)(2,1)}, f32[4,128]{1,0:T(4,128)}, f32[4,128]{1,0:T(4,128)}, f32[4,128]{1,0:T(4,128)}) custom-call(bf16[3,64,512]{2,1,0:T(8,128)(2,1)} %get-tuple-element.8.refs_0_, f32[4,128]{1,0:T(4,128)} %get-tuple-element.9.refs_1_, f32[4,128]{1,0:T(4,128)} %get-tuple-element.10.refs_2_, f32[4,128]{1,0:T(4,128)} %get-tuple-element.11.refs_3_), custom_call_target="tpu_custom_call" | custom-call | tf_op jit(solution)/shard_map/pallas_call | solution.py:652

commit v7 on v6

--- a/solution.py
+++ b/solution.py
@@ -122,10 +122,10 @@
         return send(piece, piece, self.sent.at[3], self.z_out.at[tile], self.peers["z"][d - 1])
 
     def y_up(self, d, piece):
-        return send(piece, piece, self.sent.at[4], self.y_out.at[d - 1], self.peers["y"][d - 1])
-
-    def cross_up(self, piece):
-        return send(piece, piece, self.sent.at[6], self.cross.at[0], self.peers["far"])
+        return send(piece, piece, self.sent.at[4], self.y_out.at[0], self.peers["y"][d - 1])
+
+    def cross_up(self, d, piece):
+        return send(piece, piece, self.sent.at[6], self.cross.at[0], self.peers["cross"][d - 1])
 
     def core_up(self, group):
         piece = self.out.at[self.pos[3], group]
@@ -171,9 +171,9 @@
             self.out[c, y, z] = self.acc_y[z] + sum(self.buf_z[d - 1] for d in range(1, ZS))
             for d in FAR_16:
                 self.z_up(d, z).start()
-            self.cross_up(self.out.at[c, y, z]).start()
             for d in FAR_4:
                 self.y_up(d, self.out.at[c, y, z]).start()
+                self.cross_up(d, self.out.at[c, y, z]).start()
 
     def start_y_back(self):
         _, y, z, c = self.pos
@@ -183,32 +183,28 @@
             @pl.when(source < TILES)
             def _():
                 self.z_up(d, source).wait_recv()
-                self.cross_up(self.out.at[c, y, source]).start()
                 for e in FAR_4:
                     self.y_up(e, self.out.at[c, y, source]).start()
+                    self.cross_up(e, self.out.at[c, y, source]).start()
 
     def start_core_back(self):
         _, y, _, c = self.pos
         self.core_up(y).start()
-        for d in (1, 3):
-            group = lax.rem(y + YS - d, YS)
-            self.y_up(d, self.out.at[c, group]).wait_recv()
-            self.core_up(group).start()
 
     def finish(self):
         _, y, _, c = self.pos
-        far = lax.rem(y + 2, YS)
-        self.y_up(2, self.out.at[c, far]).wait_recv()
-        arrival(self.out.at[1 - c, far], self.cross.at[0], self.sent.at[6], self.peers["far"])
-        arrival(self.buf_y, self.core_out.at[0], self.sent.at[5], self.peers["c"])
+        peer = self.peers["c"]
+        arrival(self.buf_y, self.y_out.at[0], self.sent.at[4], peer)
+        arrival(self.buf_y, self.cross.at[0], self.sent.at[6], peer)
+        arrival(self.out.at[1 - c, y], self.core_out.at[0], self.sent.at[5], peer)
 
     def drain(self):
         z, peer = self.pos[2], self.peers["c"]
         departure(self.buf_c, self.sent.at[0], self.core_in.at[0], peer)
         departure(self.buf_y, self.sent.at[1], self.y_in.at[0], peer)
         departure(self.buf_y, self.sent.at[4], self.y_in.at[0], peer)
-        departure(self.buf_y, self.sent.at[5], self.core_in.at[0], peer)
-        departure(self.acc_y, self.sent.at[6], self.core_in.at[0], peer)
+        departure(self.acc_y, self.sent.at[5], self.core_in.at[0], peer)
+        departure(self.buf_y, self.sent.at[6], self.core_in.at[0], peer)
 
         @pl.when(z < TILES)
         def _():
@@ -383,7 +379,7 @@
         "yin" + tag: dma((TILES,)),
         "zin" + tag: dma((1,)),
         "zout" + tag: dma((TILES,)),
-        "yout" + tag: dma((YS - 1,)),
+        "yout" + tag: dma((1,)),
         "coreout" + tag: dma((1,)),
     }
 
@@ -455,8 +451,8 @@
         "x": [at(lax.rem(x + d, XS), y, z, c) for d in range(1, XS)],
         "z": [at(x, y, lax.rem(z + d, ZS), c) for d in range(1, ZS)],
     }
-    peers["far"] = at(x, lax.rem(y + 2, YS), z, 1 - c)
-    everyone = [peers["c"], peers["far"]] + peers["y"] + peers["x"] + peers["z"]
+    peers["cross"] = [at(x, lax.rem(y + d, YS), z, 1 - c) for d in range(1, YS)]
+    everyone = [peers["c"]] + peers["cross"] + peers["y"] + peers["x"] + peers["z"]
     barrier = pltpu.get_barrier_semaphore()
     for target in everyone:
         pl.semaphore_signal(barrier, inc=1, device_id=target, device_id_type=MESH)

time: 89.3 us -> 88.6 us (level)
  Pallas kernels: 87.9 us -> 86.7 us
    pallas_call x1, Pallas kernels: 86.2 us -> 85 us  [shards(): pl.pallas_call(functools.partial(kernel, 1.0 / math.sqrt(total_rows)), ou...]
where the time goes in v7:
time: 88.6 us; the launch traced here: 87.9 us
  Pallas kernels  86.7 us (98%)
  between operations  1.29 us (1%)
    pallas_call x1, Pallas kernels, shards(): pl.pallas_call(functools.partial(kernel, 1.0 / math.sqrt(total_rows)), ou...  85 us

profile of v7, /device:TPU:1, one launch (start us, length us, event | category | flops | bytes accessed | tf_op | source)
XLA Modules:
  0.0 87.9 jit_solution(12823567125834129295)
XLA Ops:
  1.3 85.0 %shard_map.120 = (bf16[3,64,512]{2,1,0:T(8,128)(2,1)}, f32[4,128]{1,0:T(4,128)}, f32[4,128]{1,0:T(4,128)}, f32[4,128]{1,0:T(4,128)}) custom-call(bf16[3,64,512]{2,1,0:T(8,128)(2,1)} %x_hbm.1, bf16[3,64,512]{2,1,0:T(8,128)(2,1)} %cot_hbm.1, bf16[512,512]{1,0:T(8,128)(2,1)} %wq_hbm.1, bf16[512,512]{1,0:T(8,128)(2,1)} %wk_hbm.1, bf16[512,512]{1,0:T(8,128)(2,1)} %wv_hbm.1, ...), custom_call_target="tpu_custom_call" | custom-call | tf_op jit(solution)/shard_map/pallas_call | solution.py:640
  86.3 1.6 %shard_map.121 = (bf16[3,64,512]{2,1,0:T(8,128)(2,1)}, f32[4,128]{1,0:T(4,128)}, f32[4,128]{1,0:T(4,128)}, f32[4,128]{1,0:T(4,128)}) custom-call(bf16[3,64,512]{2,1,0:T(8,128)(2,1)} %get-tuple-element.8.refs_0_, f32[4,128]{1,0:T(4,128)} %get-tuple-element.9.refs_1_, f32[4,128]{1,0:T(4,128)} %get-tuple-element.10.refs_2_, f32[4,128]{1,0:T(4,128)} %get-tuple-element.11.refs_3_), custom_call_target="tpu_custom_call" | custom-call | tf_op jit(solution)/shard_map/pallas_call | solution.py:648
